TPU v7x, 256 devices: a whole 4x4x8 slice. The times are simulated.
256 devices in a mesh: mem: 4 (over y), sec: 64 (over x, z, core).
Axes of the slice: x: 4, y: 4, z: 8, core: 2. Of those that a mesh axis runs over, the one named last changes fastest.
Arguments:
- outer_source: float32 [8, 8192, 1024], P('mem', 'sec'), may hold values from -6 to 6
- outer_depth: float32 [8192, 1024], P('sec'), may hold values from 0.05 to 0.45
- wet_tiles: int32 [64, 8], replicated, may hold values 0 or 1
- nest_host: int32 [64], replicated, may hold values from 0 to 63, as said below
- nest_anchor: int32 [64, 2], replicated, may hold values from 0 to 960, as said below
- nest_source: float32 [8, 64, 384, 384], P('mem', 'sec'), may hold values from -6 to 6
- nest_depth: float32 [64, 384, 384], P('sec'), may hold values from 0.05 to 0.45
Outputs:
- outer_level: float32 [8, 8192, 1024], P('mem', 'sec')
- outer_flux: float32 [2, 8, 8192, 1024], P(None, 'mem', 'sec')
- peak_mean: float32 [64, 384, 384], P('sec')
- peak_var: float32 [64, 384, 384], P('sec')
Inputs may be any that keep to these rules, and one draw needn't show every extreme that they name: `nest_host`: every section holds either no nest or exactly 2 nests; sections 0 and 63 hold nests. `nest_anchor`: column 0 is at most 64 and column 1 at most 960, so that a nest's block lies within its host section; some nest reaches both.
All inputs are finite; a program needn't handle non-finite values.
Results may differ from a plain program's by a relative error of at most 0.00002.
Values sent between devices are 32-bit elements; how exact they have to be, the bound alone decides.
A program may use at most 64 MiB of HBM per device.

v0:
```python
import jax
import jax.numpy as jnp
from jax import lax
from jax.sharding import PartitionSpec as P

TILE = 128
NEST_COARSE = 64
REFINE = 6
STEPS = 3
HOST_MOST = 2


def passed_along(value, axis, steps):
    count = lax.axis_size(axis)
    initial, last = (max(0, -steps), min(count, count - steps))
    return lax.ppermute(value, axis, [(source, source + steps) for source in range(initial, last)])


def from_left(field):
    return jnp.concatenate([jnp.zeros_like(field[..., :1]), field[..., :-1]], axis=-1)


def from_right(field):
    return jnp.concatenate([field[..., 1:], jnp.zeros_like(field[..., :1])], axis=-1)


def from_above(field):
    return jnp.concatenate([jnp.zeros_like(field[..., :1, :]), field[..., :-1, :]], axis=-2)


def from_below(field):
    return jnp.concatenate([field[..., 1:, :], jnp.zeros_like(field[..., :1, :])], axis=-2)


def spread_tiles(flags):
    return jnp.broadcast_to(
        flags[:, None, :, None], (flags.shape[0], TILE, flags.shape[1], TILE)
    ).reshape(flags.shape[0] * TILE, flags.shape[1] * TILE)


def edge_cells(surface, row_start, col_start):
    zero_index = jnp.zeros((), jnp.int32)
    coarse_block = lax.dynamic_slice(
        surface, (zero_index, row_start, col_start), (surface.shape[0], NEST_COARSE, NEST_COARSE)
    )
    return jnp.concatenate(
        [
            coarse_block[:, 0, :],
            coarse_block[:, -1, :],
            coarse_block[:, :, 0],
            coarse_block[:, :, -1],
        ],
        axis=-1,
    )


def force_edges(updated, edge_values):
    width = NEST_COARSE
    row_total = updated.shape[-2]
    col_total = updated.shape[-1]
    top_edge = jnp.repeat(edge_values[..., 0:width], REFINE, axis=-1)[..., None, :]
    bottom_edge = jnp.repeat(edge_values[..., width : 2 * width], REFINE, axis=-1)[..., None, :]
    west_edge = jnp.repeat(edge_values[..., 2 * width : 3 * width], REFINE, axis=-1)[..., :, None]
    east_edge = jnp.repeat(edge_values[..., 3 * width : 4 * width], REFINE, axis=-1)[..., :, None]
    row_ids = lax.broadcasted_iota(jnp.int32, (row_total, col_total), 0)
    col_ids = lax.broadcasted_iota(jnp.int32, (row_total, col_total), 1)
    updated = jnp.where(row_ids == 0, top_edge, updated)
    updated = jnp.where(row_ids == row_total - 1, bottom_edge, updated)
    updated = jnp.where(col_ids == 0, west_edge, updated)
    updated = jnp.where(col_ids == col_total - 1, east_edge, updated)
    return updated


def nest_substep(surface, flux_x, flux_y, depth_coef, edge_values):
    updated = surface - (flux_x - from_left(flux_x)) - (flux_y - from_above(flux_y))
    updated = force_edges(updated, edge_values)
    flux_x = flux_x - depth_coef * (from_right(updated) - updated)
    flux_y = flux_y - depth_coef * (from_below(updated) - updated)
    return (updated, flux_x, flux_y)


def body(outer_source, outer_depth, wet_tiles, nest_host, nest_anchor, nest_source, nest_depth):
    section = lax.axis_index("sec")
    row_count = outer_source.shape[1]
    tile_band = row_count // TILE
    tile_flags = wet_tiles.astype(jnp.float32)
    own_flags = lax.dynamic_slice_in_dim(tile_flags, section * tile_band, tile_band, 0)
    wet_mask = spread_tiles(own_flags)
    nest_count = nest_host.shape[0]
    positions = jnp.arange(nest_count, dtype=jnp.int32)
    same_host = nest_host[:, None] == nest_host[None, :]
    host_rank = jnp.sum(
        (same_host & (positions[None, :] < positions[:, None])).astype(jnp.int32), axis=1
    )
    slot_rows = []
    slot_cols = []
    slot_used = []
    for slot_index in range(HOST_MOST):
        selected = (nest_host == section) & (host_rank == slot_index)
        slot_rows.append(jnp.sum(jnp.where(selected, nest_anchor[:, 0], 0)))
        slot_cols.append(jnp.sum(jnp.where(selected, nest_anchor[:, 1], 0)))
        slot_used.append(jnp.any(selected).astype(jnp.float32))
    host_here = lax.dynamic_index_in_dim(nest_host, section, 0, keepdims=False)
    rank_here = lax.dynamic_index_in_dim(host_rank, section, 0, keepdims=False)
    slot_pick = host_here * HOST_MOST + rank_here

    def host_slots(surface):
        return jnp.stack(
            [
                slot_used[slot_index]
                * edge_cells(surface, slot_rows[slot_index], slot_cols[slot_index])
                for slot_index in range(HOST_MOST)
            ]
        )

    fine_depth = nest_depth[0]
    surface = outer_source
    flux_x = jnp.zeros_like(surface)
    flux_y = jnp.zeros_like(surface)
    fine_start = nest_source[:, 0]
    state = (
        fine_start,
        jnp.zeros_like(fine_start),
        jnp.zeros_like(fine_start),
        jnp.full(fine_start.shape, -jnp.inf, jnp.float32),
    )
    for step_index in range(STEPS):
        advance_flux_x = flux_x
        advance_flux_y = flux_y
        top_row = passed_along(advance_flux_y[:, -1:, :], "sec", 1)
        prior_y = jnp.concatenate([top_row, advance_flux_y[:, :-1, :]], axis=1)
        updated = wet_mask * (
            surface - (advance_flux_x - from_left(advance_flux_x)) - (advance_flux_y - prior_y)
        )
        under_row = passed_along(updated[:, :1, :], "sec", -1)
        below = jnp.concatenate([updated[:, 1:, :], under_row], axis=1)
        advance_flux_x = wet_mask * (advance_flux_x - outer_depth * (from_right(updated) - updated))
        advance_flux_y = wet_mask * (advance_flux_y - outer_depth * (below - updated))
        surface = updated
        flux_x = advance_flux_x
        flux_y = advance_flux_y
        gathered = lax.all_gather(host_slots(surface), "sec", axis=0, tiled=True)
        edge_values = lax.dynamic_index_in_dim(gathered, slot_pick, 0, keepdims=False)

        def one_substep(counter, carry):
            fine_level, fine_x, fine_y, peak_level = carry
            fine_level, fine_x, fine_y = nest_substep(
                fine_level, fine_x, fine_y, fine_depth, edge_values
            )
            return (fine_level, fine_x, fine_y, jnp.maximum(peak_level, fine_level))

        state = lax.fori_loop(0, REFINE, one_substep, state)
    peak_level = state[3]
    members = peak_level.shape[0] * lax.axis_size("mem")
    member_total = lax.psum(jnp.sum(peak_level, axis=0), "mem")
    member_mean = member_total / members
    deviation = peak_level - member_mean
    spread = lax.psum(jnp.sum(deviation * deviation, axis=0), "mem")
    member_var = spread / members
    return (surface, jnp.stack([flux_x, flux_y]), member_mean[None], member_var[None])


def solution(mesh):
    return jax.shard_map(
        body,
        mesh=mesh,
        in_specs=(
            P("mem", "sec", None),
            P("sec", None),
            P(),
            P(),
            P(),
            P("mem", "sec", None, None),
            P("sec", None, None),
        ),
        out_specs=(
            P("mem", "sec", None),
            P(None, "mem", "sec", None),
            P("sec", None, None),
            P("sec", None, None),
        ),
        check_vma=False,
    )
```

profile of v0, /device:TPU:1, one launch (start us, length us, event | category | flops | bytes accessed | tf_op | source)
XLA Modules:
  0.0 531.0 jit_solution(17363709002181831836)
XLA Ops:
  7.3 5.1 collective-permute-start
  26.0 1.9 collective-permute-start.1
  28.4 47.5 %all_gather.9 = f32[128,2,256]{2,1,0:T(2,128)S(1)} all-gather(f32[2,2,256]{2,1,0:T(2,128)S(1)} %pad_maximum_fusion.1), channel_id=1, replica_groups=mesh['mem'=4,'sec'=64] {'sec'}, dimensions={0}, use_global_device_ids=true | all-gather | bytes 266240 | tf_op jit(solution)/shard_map/all_gather | solution.py:142
  80.5 2.5 collective-permute-start.2
  83.0 78.4 %while.51 = (s32[]{:T(128)}, f32[2,384,384]{2,1,0:T(8,128)S(1)}, f32[2,384,384]{2,1,0:T(8,128)S(1)}, f32[2,384,384]{2,1,0:T(8,128)S(1)}, f32[2,384,384]{2,1,0:T(...) while((s32[]{:T(128)}, f32[2,384,384]{2,1,0:T(8,128)S(1)}, ...), condition=%wide.region_8.9_spmd.clone, body=%wide.region_7.8_spmd.clone.sunk | while | flops 5309187 | bytes 39570220 | solution.py:152
  161.5 3.2 fusion.4
  165.1 2.4 collective-permute-start.3
  168.1 1.9 collective-permute-done.3
  171.0 2.5 collective-permute-start.4
  173.5 45.4 %all_gather.10 = f32[128,2,256]{2,1,0:T(2,128)S(1)} all-gather(f32[2,2,256]{2,1,0:T(2,128)S(1)} %pad_maximum_fusion.2), channel_id=1, replica_groups=mesh['mem'=4,'sec'=64] {'sec'}, dimensions={0}, use_global_device_ids=true | all-gather | bytes 266240 | tf_op jit(solution)/shard_map/all_gather | solution.py:142
  220.8 41.7 %all_gather.11 = f32[128,2,256]{2,1,0:T(2,128)S(1)} all-gather(f32[2,2,256]{2,1,0:T(2,128)S(1)} %pad_maximum_fusion.3), channel_id=1, replica_groups=mesh['mem'=4,'sec'=64] {'sec'}, dimensions={0}, use_global_device_ids=true | all-gather | bytes 266240 | tf_op jit(solution)/shard_map/all_gather | solution.py:142
  263.1 77.5 %while.49 = (s32[]{:T(128)}, f32[2,384,384]{2,1,0:T(8,128)S(1)}, f32[2,384,384]{2,1,0:T(8,128)S(1)}, f32[2,384,384]{2,1,0:T(8,128)S(1)}, f32[2,384,384]{2,1,0:T(...) while((s32[]{:T(128)}, f32[2,384,384]{2,1,0:T(8,128)S(1)}, ...), condition=%wide.region_10.11_spmd, body=%wide.region_9.10_spmd.sunk | while | flops 4424450 | bytes 25411240 | solution.py:152
  270.5 3.3 fusion.37
  283.4 3.3 fusion.37
  296.3 3.3 fusion.37
  309.3 3.3 fusion.37
  322.2 3.3 fusion.37
  335.1 3.3 fusion.37
  340.6 81.9 %while.50 = (s32[]{:T(128)}, f32[2,384,384]{2,1,0:T(8,128)S(1)}, f32[2,384,384]{2,1,0:T(8,128)S(1)}, f32[2,384,384]{2,1,0:T(8,128)S(1)}, f32[2,384,384]{2,1,0:T(...) while((s32[]{:T(128)}, f32[2,384,384]{2,1,0:T(8,128)S(1)}, ...), condition=%wide.region_12.13_spmd, body=%wide.region_11.12_spmd.sunk | while | flops 4424450 | bytes 25394800 | solution.py:152
  348.8 3.3 fusion.39
  362.4 3.3 fusion.39
  376.1 3.3 fusion.39
  389.7 3.3 fusion.39
  403.4 3.3 fusion.39
  417.0 3.3 fusion.39
  422.5 2.2 reduce_sum.68
  424.8 45.2 %all-reduce.21.cloned.1.call-done = f32[384,384]{1,0:T(8,128)} async-done(((f32[384,384]{1,0:T(8,128)}), f32[384,384]{1,0:T(8,128)}) %all-reduce.21.cloned.1.call-update) | async-done | bytes 589840 | tf_op jit(solution)/shard_map/psum | solution.py:155
  469.9 2.0 broadcast_multiply_fusion
  473.3 4.4 collective-permute-start.5
  478.2 2.0 collective-permute-done.5
  482.5 39.7 %all-reduce.23.cloned.1.call-done = f32[384,384]{1,0:T(8,128)} async-done(((f32[384,384]{1,0:T(8,128)}), f32[384,384]{1,0:T(8,128)}) %all-reduce.23.cloned.1.call-update) | async-done | bytes 589840 | tf_op jit(solution)/shard_map/psum | solution.py:158
  522.3 1.9 multiply_bitcast_fusion.1
  (478 shorter events, 214.2 us)
Async XLA Ops:
  7.2 18.7 %copy-start.16 = (f32[2,128,1024]{2,1,0:T(8,128)S(1)}, f32[2,128,1024]{2,1,0:T(8,128)}, u32[]{:S(2)}) copy-start(f32[2,128,1024]{2,1,0:T(8,128)} %param.13) | copy-start | bytes 3145732
  7.2 6.0 %copy-start.31 = (s32[64,8]{0,1:T(8,128)S(1)}, s32[64,8]{0,1:T(8,128)}, u32[]{:S(2)}) copy-start(s32[64,8]{0,1:T(8,128)} %param.15) | copy-start | bytes 6148
  7.2 5.2 copy-start.33
  7.2 6.3 %copy-start.32 = (s32[64,2]{0,1:T(2,128)S(1)}, s32[64,2]{0,1:T(2,128)}, u32[]{:S(2)}) copy-start(s32[64,2]{0,1:T(2,128)} %param.17) | copy-start | bytes 1540
  7.2 462.7 %all-reduce.21.cloned.1.call-start = ((), (), s32[]{:S(2)}) async-start(), calls=%async_computation | async-start | bytes 1179648 | tf_op jit(solution)/shard_map/psum | solution.py:155
  7.3 18.5 %collective-permute-start = (f32[2,1,1024]{2,1,0:T(1,128)S(1)}, f32[2,1,1024]{2,1,0:T(1,128)S(1)}, u32[]{:S(2)}, u32[]{:S(2)}) collective-permute-start(f32[2,1,1024]{2,1,0:T(1,128)S(1)} %slice.202), channel_id=1, source_target_pairs={{0,1},{1,2},{2,3},{3,4},{4,5},{5,6},{6,7},{7,8},{8,9},{9,10},{10,1... | collective-permute-start | bytes 24584 | tf_op jit(solution)/shard_map/ppermute | solution.py:16
  13.4 63.0 %copy-start.25 = (f32[1024]{0:T(1024)}, f32[1024]{0:T(1024)S(1)}, u32[]{:S(2)}) copy-start(f32[1024]{0:T(1024)S(1)} %broadcast_bitcast_fusion) | copy-start | bytes 12292
  25.8 50.6 %copy-start.28 = (f32[2,1,1024]{2,1,0:T(1,128)}, f32[2,1,1024]{2,1,0:T(1,128)S(1)}, u32[]{:S(2)}) copy-start(f32[2,1,1024]{2,1,0:T(1,128)S(1)} %collective-permute-done) | copy-start | bytes 24580
  26.0 50.5 %collective-permute-start.1 = (f32[2,1,1024]{2,1,0:T(1,128)S(1)}, f32[2,1,1024]{2,1,0:T(1,128)S(1)}, u32[]{:S(2)}, u32[]{:S(2)}) collective-permute-start(f32[2,1,1024]{2,1,0:T(1,128)S(1)} %slice.263), channel_id=1, source_target_pairs={{1,0},{2,1},{3,2},{4,3},{5,4},{6,5},{7,6},{8,7},{9,8},{10,9},{11,1... | collective-permute-start | bytes 24584 | tf_op jit(solution)/shard_map/ppermute | solution.py:16
  76.1 1.3 copy-start.18
  76.4 6.6 %copy-start = (f32[2,1,384,384]{3,2,1,0:T(8,128)S(1)}, f32[2,1,384,384]{3,2,1,0:T(8,128)}, u32[]{:S(2)}) copy-start(f32[2,1,384,384]{3,2,1,0:T(8,128)} %param.18) | copy-start | bytes 3538948
  80.5 81.0 %collective-permute-start.2 = (f32[2,1,1024]{2,1,0:T(1,128)}, f32[2,1,1024]{2,1,0:T(1,128)}, u32[]{:S(2)}, u32[]{:S(2)}) collective-permute-start(f32[2,1,1024]{2,1,0:T(1,128)} %slice.264), channel_id=1, source_target_pairs={{0,1},{1,2},{2,3},{3,4},{4,5},{5,6},{6,7},{7,8},{8,9},{9,10},{10,1... | collective-permute-start | bytes 24584 | tf_op jit(solution)/shard_map/ppermute | solution.py:16
  116.6 1.3 copy-start.1
  129.7 1.3 copy-start.1
  142.7 1.3 copy-start.1
  155.8 1.3 copy-start.1
  165.1 5.0 collective-permute-start.3
  167.6 2.4 copy-start.19
  167.6 2.4 copy-start.26
  167.8 2.3 copy-start.12
  167.8 2.3 copy-start.15
  170.9 48.4 %copy-start.9 = (f32[2,128,1024]{2,1,0:T(8,128)}, f32[2,128,1024]{2,1,0:T(8,128)S(1)}, u32[]{:S(2)}) copy-start(f32[2,128,1024]{2,1,0:T(8,128)S(1)} %get-tuple-element.253) | copy-start | bytes 3145732
  170.9 48.4 %copy-start.13 = (f32[2,128,1024]{2,1,0:T(8,128)}, f32[2,128,1024]{2,1,0:T(8,128)S(1)}, u32[]{:S(2)}) copy-start(f32[2,128,1024]{2,1,0:T(8,128)S(1)} %get-tuple-element.252) | copy-start | bytes 3145732
  171.0 47.9 %collective-permute-start.4 = (f32[2,1,1024]{2,1,0:T(1,128)S(1)}, f32[2,1,1024]{2,1,0:T(1,128)S(1)}, u32[]{:S(2)}, u32[]{:S(2)}) collective-permute-start(f32[2,1,1024]{2,1,0:T(1,128)S(1)} %slice.270), channel_id=1, source_target_pairs={{0,1},{1,2},{2,3},{3,4},{4,5},{5,6},{6,7},{7,8},{8,9},{9,10},{10,1... | collective-permute-start | bytes 24584 | tf_op jit(solution)/shard_map/ppermute | solution.py:16
  424.7 47.2 %copy-start.3 = (f32[2,384,384]{2,1,0:T(8,128)S(1)}, f32[2,384,384]{2,1,0:T(8,128)}, u32[]{:S(2)}) copy-start(f32[2,384,384]{2,1,0:T(8,128)} %get-tuple-element.129) | copy-start | bytes 3538948
  424.7 97.5 %all-reduce.23.cloned.1.call-start = ((), (), s32[]{:S(2)}) async-start(), calls=%async_computation.1 | async-start | bytes 1179648 | tf_op jit(solution)/shard_map/psum | solution.py:158
  471.9 1.4 copy-start.8
  471.9 8.3 %copy-start.27 = (f32[1024]{0:T(1024)S(1)}, f32[1024]{0:T(1024)}, u32[]{:S(2)}) copy-start(f32[1024]{0:T(1024)} %copy-done.25) | copy-start | bytes 12292
  473.3 6.8 %collective-permute-start.5 = (f32[2,1,1024]{2,1,0:T(1,128)S(1)}, f32[2,1,1024]{2,1,0:T(1,128)S(1)}, u32[]{:S(2)}, u32[]{:S(2)}) collective-permute-start(f32[2,1,1024]{2,1,0:T(1,128)S(1)} %slice.274), channel_id=1, source_target_pairs={{1,0},{2,1},{3,2},{4,3},{5,4},{6,5},{7,6},{8,7},{9,8},{10,9},{11,1... | collective-permute-start | bytes 24584 | tf_op jit(solution)/shard_map/ppermute | solution.py:16
  477.7 2.5 copy-start.20
  477.9 2.3 copy-start.10
  477.9 2.3 copy-start.14
  (65 other events, 63.3 us)
Sparse Core Ops, SparseCore 0:
  424.8 45.0 all-reduce.20
  473.0 49.2 all-reduce.22
where the time goes:
time: 537 us; the launch traced here: 531 us
  local copies, waits for them, and re-layouts  172 us (32%)
  blocking collectives  135 us (25%)
  other arithmetic  90.5 us (17%)
  waiting for transfers between devices  88.8 us (17%)
  between operations  24.9 us (5%)
  starting transfers between devices  18.8 us (4%)
    all_gather x3, blocking collectives, body(): gathered = lax.all_gather(host_slots(surface), 'sec', axis=0, tiled=True)  135 us
    max x18, other arithmetic, one_substep(): return (fine_level, fine_x, fine_y, jnp.maximum(peak_level, fine_level))  48 us
    psum x1, waiting for transfers between devices, body(): member_total = lax.psum(jnp.sum(peak_level, axis=0), 'mem')  45.2 us
    psum x1, waiting for transfers between devices, body(): spread = lax.psum(jnp.sum(deviation * deviation, axis=0), 'mem')  39.7 us
    while x132, local copies, waits for them, and re-layouts  28 us
    ppermute x6, starting transfers between devices, passed_along(): lax.ppermute(value, axis, [(source, source + steps) for source in range(i...  18.7 us
    broadcast_in_dim x18, local copies, waits for them, and re-layouts, force_edges(): updated = jnp.where(row_ids == 0, top_edge, updated)  17.5 us
    broadcast_in_dim x18, local copies, waits for them, and re-layouts, force_edges(): updated = jnp.where(row_ids == row_total - 1, bottom_edge, updated)  17.5 us
  transfers between devices with their start and end apart: 8, of which 4 were waited for; matrix products, arithmetic and copies ran while one was open for 13% of the time, Pallas kernels for 0%

commit v1 on v0

v1 whole, which is shorter than its diff:
```python
import jax
import jax.numpy as jnp
from jax import lax
from jax.experimental import pallas as pl
from jax.experimental.pallas import tpu as pltpu
from jax.sharding import PartitionSpec as P

MESH = pl.DeviceIdType.MESH
STEPS = 3
REFINE = 6
SECTIONS = 64
X_PLANES = 4
Z_CORES = 16
STRIP = 48
VMEM = pltpu.VMEM
ANY = pl.ANY


def vmem_spec():
    return pl.BlockSpec(memory_space=pltpu.VMEM)


def smem_spec():
    return pl.BlockSpec(memory_space=pltpu.SMEM)


def any_spec():
    return pl.BlockSpec(memory_space=pl.ANY)


def halo_kernel(eta_ref, depth_ref, up_eta, dn_eta, up_depth, dn_depth, send_sem, recv_sem):
    me = lax.axis_index("sec")
    below = lax.rem(me + 1, SECTIONS)
    above = lax.rem(me + SECTIONS - 1, SECTIONS)
    barrier = pltpu.get_barrier_semaphore()
    for peer in (below, above):
        pl.semaphore_signal(barrier, inc=1, device_id={"sec": peer}, device_id_type=MESH)
    pl.semaphore_wait(barrier, 2)
    plan = (
        (eta_ref.at[:, 15], up_eta, below),
        (eta_ref.at[:, 0], dn_eta, above),
        (depth_ref.at[15], up_depth, below),
        (depth_ref.at[0], dn_depth, above),
    )
    copies = []
    for number, (source, target, peer) in enumerate(plan):
        copy = pltpu.make_async_remote_copy(
            src_ref=source,
            dst_ref=target,
            send_sem=send_sem.at[number],
            recv_sem=recv_sem.at[number],
            device_id={"sec": peer},
            device_id_type=MESH,
        )
        copy.start()
        copies.append(copy)
    for copy in copies:
        copy.wait()


def exchange_halos(eta, depth):
    rows = jax.ShapeDtypeStruct((2, 8, 1024), jnp.float32)
    coef = jax.ShapeDtypeStruct((8, 1024), jnp.float32)
    return pl.pallas_call(
        halo_kernel,
        out_shape=(rows, rows, coef, coef),
        in_specs=[any_spec()] * 2,
        out_specs=(any_spec(),) * 4,
        scratch_shapes=[pltpu.SemaphoreType.DMA((4,)), pltpu.SemaphoreType.DMA((4,))],
        compiler_params=pltpu.CompilerParams(collective_id=0, has_side_effects=True),
        name="halo",
    )(eta, depth)


def outer_kernel(
    wet_ref, host_ref, anchor_ref, eta_in, depth_in, up_eta, dn_eta, up_depth, dn_depth,
    level_ref, flux_ref, edges_ref, pick_ref,
    eta, fx, fy, dw, masks, first, last,
):
    section = lax.axis_index("sec")
    lanes = lax.broadcasted_iota(jnp.int32, (8, 1024), 1)
    subs = lax.broadcasted_iota(jnp.int32, (8, 1024), 0)

    first[section] = 0
    last[section] = 0

    def note(n, _):
        last[host_ref[n]] = n
        first[host_ref[SECTIONS - 1 - n]] = SECTIONS - 1 - n
        return 0

    lax.fori_loop(0, SECTIONS, note, 0)

    def choose(n, _):
        host = host_ref[n]
        pick_ref[n] = (host // Z_CORES) * 2 + jnp.where(first[host] == n, 0, 1)
        return 0

    lax.fori_loop(0, SECTIONS, choose, 0)

    for band in range(3):
        row = section + band - 1
        inside = (row >= 0) & (row < SECTIONS)
        row = jnp.clip(row, 0, SECTIONS - 1)
        for tile in range(8):
            flag = jnp.where(inside, wet_ref[row, tile], 0)
            masks[band, :, tile * 128 : (tile + 1) * 128] = jnp.full(
                (8, 128), flag, jnp.int32
            ).astype(jnp.float32)
    zeros = jnp.zeros((8, 1024), jnp.float32)
    masks[3] = zeros

    def band_of(k):
        return jnp.where(k == 1, 0, jnp.where(k <= 17, 1, jnp.where(k == 18, 2, 3)))

    for k, (rows, coef) in ((1, (up_eta, up_depth)), (18, (dn_eta, dn_depth))):
        mask = masks[0 if k == 1 else 2]
        dw[k] = mask * coef[...]
        for m in range(2):
            eta[m, k] = mask * rows[m]
    dw[0] = zeros
    for m in range(2):
        for k in (0, 19):
            eta[m, k] = zeros
            fx[m, k] = zeros
        fy[m, 0] = zeros
        fy[m, 19] = zeros
    dw[19] = zeros

    def fill(k, _):
        mask = masks[1]
        dw[k + 2] = mask * depth_in[k]
        for m in range(2):
            eta[m, k + 2] = mask * eta_in[m, k]
        return 0

    lax.fori_loop(0, 16, fill, 0)

    def east(x):
        return jnp.where(lanes == 1023, 0.0, pltpu.roll(x, 1023, 1))

    def west(x):
        return jnp.where(lanes == 0, 0.0, pltpu.roll(x, 1, 1))

    def south(x, following):
        return jnp.where(subs == 7, pltpu.roll(following, 7, 0), pltpu.roll(x, 7, 0))

    def north(x, previous):
        return jnp.where(subs == 0, pltpu.roll(previous, 1, 0), pltpu.roll(x, 1, 0))

    def sweep_first(k, _):
        for m in range(2):
            now = eta[m, k]
            before = eta[m, k - 1]
            fx[m, k] = -(dw[k] * (east(now) - now))
            fy[m, k - 1] = -(dw[k - 1] * (south(before, now) - before))
        return 0

    def edges(step):
        rows128 = (
            lax.broadcasted_iota(jnp.int32, (16, 8, 128), 0) * 8
            + lax.broadcasted_iota(jnp.int32, (16, 8, 128), 1)
        )
        lane16 = lax.broadcasted_iota(jnp.int32, (16, 8, 128), 2)
        lane_row = lax.broadcasted_iota(jnp.int32, (8, 128), 1)
        for slot in range(2):
            nest = (first if slot == 0 else last)[section]
            r0 = anchor_ref[nest, 0]
            c0 = anchor_ref[nest, 1]
            base = pl.multiple_of(jnp.minimum(c0 // 128, 6) * 128, 128)
            left = pl.multiple_of((c0 // 128) * 128, 128)
            right = pl.multiple_of(((c0 + 63) // 128) * 128, 128)
            for m in range(2):

                def row_of(r):
                    tile = r // 8 + 2
                    x = eta[m, tile, pl.ds(lax.rem(r, 8), 1), pl.ds(base, 256)]
                    return jnp.broadcast_to(x, (8, 256))

                shift = c0 - base
                top = pltpu.roll(row_of(r0), 256 - shift, 1)[:, :128]
                bottom = pltpu.roll(row_of(r0 + 63), lax.rem(320 - shift, 256), 1)[:, :128]
                pair = jnp.where(lane_row < 64, top, bottom)
                at = (step * 2 + m) * 2
                edges_ref[slot, at : at + 1, :] = pair[0:1]
                west_block = eta[m, 2:18, :, pl.ds(left, 128)]
                east_block = eta[m, 2:18, :, pl.ds(right, 128)]
                west_col = jnp.sum(jnp.where(lane16 == c0 - left, west_block, 0.0), axis=2, keepdims=True)
                east_col = jnp.sum(jnp.where(lane16 == c0 + 63 - right, east_block, 0.0), axis=2, keepdims=True)
                place = rows128 - r0
                both = jnp.where((lane16 == place) & (lane16 < 64), west_col, 0.0) + jnp.where(
                    (lane16 == place + 64) & (lane16 >= 64), east_col, 0.0
                )
                edges_ref[slot, at + 1 : at + 2, :] = jnp.sum(jnp.sum(both, axis=0), axis=0, keepdims=True)

    for slot in range(2):
        edges_ref[slot, 12:16, :] = jnp.zeros((4, 128), jnp.float32)
    lax.fori_loop(1, 20, sweep_first, 0)
    edges(0)

    def full_step(step):
        def body(k, carry):
            new_carry = []
            mask = masks[band_of(k)]
            for m in range(2):
                px = fx[m, k]
                py = fy[m, k]
                py_before = carry[m]
                before = eta[m, k - 1]
                now = mask * (eta[m, k] - (px - west(px)) - (py - north(py, py_before)))
                eta[m, k] = now
                fx[m, k] = px - dw[k] * (east(now) - now)
                fy[m, k - 1] = py_before - dw[k - 1] * (south(before, now) - before)
                new_carry.append(py)
            return tuple(new_carry)

        lax.fori_loop(1, 20, body, (zeros, zeros))
        edges(step)

    full_step(1)
    full_step(2)

    def emit(k, _):
        for m in range(2):
            level_ref[m, k] = eta[m, k + 2]
            flux_ref[0, m, k] = fx[m, k + 2]
            flux_ref[1, m, k] = fy[m, k + 2]
        return 0

    lax.fori_loop(0, 16, emit, 0)


def outer_steps(wet_tiles, nest_host, nest_anchor, eta, depth, halos):
    return pl.pallas_call(
        outer_kernel,
        out_shape=(
            jax.ShapeDtypeStruct((2, 16, 8, 1024), jnp.float32),
            jax.ShapeDtypeStruct((2, 2, 16, 8, 1024), jnp.float32),
            jax.ShapeDtypeStruct((2, 16, 128), jnp.float32),
            jax.ShapeDtypeStruct((SECTIONS,), jnp.int32),
        ),
        in_specs=[smem_spec()] * 3 + [vmem_spec()] * 6,
        out_specs=(vmem_spec(), vmem_spec(), vmem_spec(), smem_spec()),
        scratch_shapes=[
            VMEM((2, 20, 8, 1024), jnp.float32),
            VMEM((2, 20, 8, 1024), jnp.float32),
            VMEM((2, 20, 8, 1024), jnp.float32),
            VMEM((20, 8, 1024), jnp.float32),
            VMEM((4, 8, 1024), jnp.float32),
            pltpu.SMEM((SECTIONS,), jnp.int32),
            pltpu.SMEM((SECTIONS,), jnp.int32),
        ],
        compiler_params=pltpu.CompilerParams(vmem_limit_bytes=40 << 20),
        name="outer",
    )(wet_tiles, nest_host, nest_anchor, eta, depth, *halos)


def route_kernel(
    host_ref, pick_ref, edges_ref, out_ref,
    gathered, outgoing, incoming, send_x, recv_x, send_z, recv_z,
):
    me = lax.axis_index("sec")
    plane = me // Z_CORES
    spot = lax.rem(me, Z_CORES)
    barrier = pltpu.get_barrier_semaphore()
    for step in range(1, X_PLANES):
        peer = lax.rem(plane + step, X_PLANES) * Z_CORES + spot
        pl.semaphore_signal(barrier, inc=1, device_id={"sec": peer}, device_id_type=MESH)
    for step in range(1, Z_CORES):
        peer = plane * Z_CORES + lax.rem(spot + step, Z_CORES)
        pl.semaphore_signal(barrier, inc=1, device_id={"sec": peer}, device_id_type=MESH)
    gathered[plane] = edges_ref[...]
    pl.semaphore_wait(barrier, X_PLANES + Z_CORES - 2)

    copies = []
    for step in range(1, X_PLANES):
        peer = lax.rem(plane + step, X_PLANES) * Z_CORES + spot
        copy = pltpu.make_async_remote_copy(
            src_ref=edges_ref,
            dst_ref=gathered.at[plane],
            send_sem=send_x.at[step - 1],
            recv_sem=recv_x.at[step - 1],
            device_id={"sec": peer},
            device_id_type=MESH,
        )
        copy.start()
        copies.append(copy)
    for copy in copies:
        copy.wait()

    second = []
    for step in range(Z_CORES):
        target = lax.rem(spot + step, Z_CORES)
        choice = pick_ref[plane * Z_CORES + target]
        message = gathered[choice // 2, lax.rem(choice, 2)]
        if step == 0:
            incoming[spot] = message
            continue
        outgoing[step] = message
        copy = pltpu.make_async_remote_copy(
            src_ref=outgoing.at[step],
            dst_ref=incoming.at[spot],
            send_sem=send_z.at[step - 1],
            recv_sem=recv_z.at[step - 1],
            device_id={"sec": plane * Z_CORES + target},
            device_id_type=MESH,
        )
        copy.start()
        second.append(copy)
    for copy in second:
        copy.wait()
    out_ref[...] = incoming[lax.rem(host_ref[me], Z_CORES)]


def route_edges(nest_host, pick, edges):
    return pl.pallas_call(
        route_kernel,
        out_shape=jax.ShapeDtypeStruct((16, 128), jnp.float32),
        in_specs=[smem_spec(), smem_spec(), vmem_spec()],
        out_specs=vmem_spec(),
        scratch_shapes=[
            VMEM((X_PLANES, 2, 16, 128), jnp.float32),
            VMEM((Z_CORES, 16, 128), jnp.float32),
            VMEM((Z_CORES, 16, 128), jnp.float32),
            pltpu.SemaphoreType.DMA((X_PLANES - 1,)),
            pltpu.SemaphoreType.DMA((X_PLANES - 1,)),
            pltpu.SemaphoreType.DMA((Z_CORES - 1,)),
            pltpu.SemaphoreType.DMA((Z_CORES - 1,)),
        ],
        compiler_params=pltpu.CompilerParams(collective_id=1, has_side_effects=True),
        name="route",
    )(nest_host, pick, edges)


def nest_kernel(edge_ref, source_ref, depth_ref, peak_ref, h, div, peak, coef, cols, rows, src, dsrc, sem):
    copies = []
    for t in range(3):
        part = pl.ds(128 * t, 128)
        for m in range(2):
            copies.append(
                pltpu.make_async_copy(source_ref.at[m, 0, :, part], src.at[m, t], sem.at[3 * m + t])
            )
        copies.append(pltpu.make_async_copy(depth_ref.at[0, :, part], dsrc.at[t], sem.at[6 + t]))
    for copy in copies:
        copy.start()

    lane = lax.broadcasted_iota(jnp.int32, (8, 128), 1)
    sub = lax.broadcasted_iota(jnp.int32, (8, 128), 0)

    def spread(row, index):
        wide = jnp.broadcast_to(row, (8, 128))
        return jnp.take_along_axis(wide, index, axis=1)

    for step in range(STEPS):
        for m in range(2):
            at = (step * 2 + m) * 2
            level = edge_ref[at : at + 1, :]
            upright = edge_ref[at + 1 : at + 2, :]
            for q in range(8):
                cols[step, m, 0, q] = spread(upright, sub * 8 + q)
                cols[step, m, 1, q] = spread(upright, sub * 8 + q + 64)
            for side in range(2):
                for t in range(3):
                    value = spread(level, (lane + 128 * t) // REFINE + 64 * side)
                    if t == 0:
                        value = jnp.where(lane == 0, cols[step, m, 0, 7 * side], value)
                    if t == 2:
                        value = jnp.where(lane == 127, cols[step, m, 1, 7 * side], value)
                    rows[step, m, side, t] = value

    def force(value, step, m, t, i, side):
        if side is not None:
            edge_sub = 0 if side == 0 else 7
            value = jnp.where(sub == edge_sub, rows[step, m, side, t], value)
        if t == 0:
            value = jnp.where(lane == 0, cols[step, m, 0, i // REFINE], value)
        if t == 2:
            value = jnp.where(lane == 127, cols[step, m, 1, i // REFINE], value)
        return value

    for copy in copies:
        copy.wait()

    def load(i, side=None):
        for t in range(3):
            coef[i, t] = dsrc[t, pl.ds(i, 8, stride=STRIP), :]
            for m in range(2):
                value = force(src[m, t, pl.ds(i, 8, stride=STRIP), :], 0, m, t, i, side)
                h[m, i, t] = value
                peak[m, i, t] = value
                div[m, i, t] = jnp.zeros((8, 128), jnp.float32)

    load(0, 0)

    def load_body(i, _):
        load(i)
        return 0

    lax.fori_loop(1, STRIP - 1, load_body, 0)
    load(STRIP - 1, 1)

    def advance(i, step, carry, side=None, last=False):
        out = []
        for m in range(2):
            now, above = carry[m]
            following = [h[m, i + 1, t] for t in range(3)]
            lefts = [pltpu.roll(now[t], 127, 1) for t in range(3)]
            f = []
            for t in range(3):
                ahead = lefts[t] if t == 2 else jnp.where(lane == 127, lefts[t + 1], lefts[t])
                f.append(coef[i, t] * (ahead - now[t]))
            rights = [pltpu.roll(f[t], 1, 1) for t in range(3)]
            g = []
            for t in range(3):
                behind = rights[t] if t == 0 else jnp.where(lane == 0, rights[t - 1], rights[t])
                g.append(coef[i, t] * (following[t] - now[t]))
                change = div[m, i, t] - ((f[t] - behind) + (g[t] - above[t]))
                value = force(now[t] - change, step, m, t, i, side)
                div[m, i, t] = change
                h[m, i, t] = value
                peak[m, i, t] = jnp.maximum(peak[m, i, t], value)
            out.append((following, g))
        return out

    def substep(k, _):
        step = k // REFINE
        carry = []
        for m in range(2):
            now = [h[m, 0, t] for t in range(3)]
            above = []
            for t in range(3):
                wrapped = pltpu.roll(now[t], 7, 0)
                h[m, STRIP, t] = wrapped
                above.append(
                    pltpu.roll(coef[STRIP - 1, t] * (wrapped - h[m, STRIP - 1, t]), 1, 0)
                )
            carry.append((now, above))
        carry = advance(0, step, carry, side=0)
        carry = lax.fori_loop(1, STRIP - 1, lambda i, c: advance(i, step, c), carry, unroll=2)
        advance(STRIP - 1, step, carry, side=1)
        return 0

    lax.fori_loop(1, STEPS * REFINE, substep, 0)

    def store(i, _):
        for m in range(2):
            for t in range(3):
                peak_ref[m, t, pl.ds(i, 8, stride=STRIP), :] = peak[m, i, t]
        return 0

    lax.fori_loop(0, STRIP, store, 0)


def advance_nests(edges, source, depth):
    return pl.pallas_call(
        nest_kernel,
        out_shape=jax.ShapeDtypeStruct((2, 3, 384, 128), jnp.float32),
        in_specs=[vmem_spec(), any_spec(), any_spec()],
        out_specs=vmem_spec(),
        scratch_shapes=[
            VMEM((2, STRIP + 1, 3, 8, 128), jnp.float32),
            VMEM((2, STRIP, 3, 8, 128), jnp.float32),
            VMEM((2, STRIP, 3, 8, 128), jnp.float32),
            VMEM((STRIP, 3, 8, 128), jnp.float32),
            VMEM((STEPS, 2, 2, 8, 8, 128), jnp.float32),
            VMEM((STEPS, 2, 2, 3, 8, 128), jnp.float32),
            VMEM((2, 3, 384, 128), jnp.float32),
            VMEM((3, 384, 128), jnp.float32),
            pltpu.SemaphoreType.DMA((9,)),
        ],
        compiler_params=pltpu.CompilerParams(vmem_limit_bytes=40 << 20),
        name="nests",
    )(edges, source, depth)


def reduce_kernel(peak_ref, mean_ref, var_ref, r1, st, r2, mv, s1, q1, s2, q2, s3, q3, s4, q4, osem):
    m = lax.axis_index("mem")
    near = m + 1 - 2 * lax.rem(m, 2)
    far = 3 - m
    high = m // 2
    gray = lax.rem(lax.rem(m, 2) + high, 2)
    barrier = pltpu.get_barrier_semaphore()
    for peer in (near, far):
        pl.semaphore_signal(barrier, inc=1, device_id={"mem": peer}, device_id_type=MESH)
    pl.semaphore_wait(barrier, 2)

    one = (near, far)
    two = (far, near)
    keep1 = (gray, high)
    keep2 = (high, gray)

    def rows_of(half, bit1):
        return pl.multiple_of(half * 192 + bit1 * 96, 8)

    def remote(src, dst, send, recv, peer):
        return pltpu.make_async_remote_copy(
            src_ref=src, dst_ref=dst, send_sem=send, recv_sem=recv,
            device_id={"mem": peer}, device_id_type=MESH,
        )

    flows = [(t, half) for t in range(3) for half in range(2)]
    first = {}
    for t, half in flows:
        n = 2 * t + half
        away = pl.ds(rows_of(half, 1 - keep1[half]), 96)
        first[n] = remote(peak_ref.at[:, t, away, :], r1.at[n], s1.at[n], q1.at[n], one[half])
        first[n].start()

    second = {}
    for t, half in flows:
        n = 2 * t + half
        first[n].wait_recv()
        kept = rows_of(half, keep1[half])

        def merge(index, part, n=n, t=t, kept=kept):
            local = pl.multiple_of(part * 48 + index * 8, 8)
            here = pl.ds(pl.multiple_of(kept + local, 8), 8)
            a = peak_ref[0, t, here, :]
            b = peak_ref[1, t, here, :]
            c = r1[n, 0, pl.ds(local, 8), :]
            d = r1[n, 1, pl.ds(local, 8), :]
            total = (a + b) + (c + d)
            middle = total * 0.25
            a = a - middle
            b = b - middle
            c = c - middle
            d = d - middle
            st[n, 0, pl.ds(local, 8), :] = total
            st[n, 1, pl.ds(local, 8), :] = (a * a + b * b) + (c * c + d * d)

        def merge_part(part):
            lax.fori_loop(0, 6, lambda index, _: (merge(index, part), 0)[1], 0)

        merge_part(1 - keep2[half])
        away = pl.ds(pl.multiple_of((1 - keep2[half]) * 48, 8), 48)
        second[n] = remote(st.at[n, :, away, :], r2.at[n], s2.at[n], q2.at[n], two[half])
        second[n].start()
        merge_part(keep2[half])

    third = {}
    for t, half in flows:
        n = 2 * t + half
        second[n].wait_recv()
        kept = rows_of(half, keep1[half])

        def finish(index, _, n=n, t=t, kept=kept, half=half):
            offset = pl.multiple_of(index * 8, 8)
            local = pl.multiple_of(keep2[half] * 48 + offset, 8)
            own = st[n, 0, pl.ds(local, 8), :]
            other = r2[n, 0, pl.ds(offset, 8), :]
            gap = own - other
            squares = (st[n, 1, pl.ds(local, 8), :] + r2[n, 1, pl.ds(offset, 8), :]) + gap * gap * 0.125
            here = pl.ds(pl.multiple_of(kept + local, 8), 8)
            mv[0, t, here, :] = (own + other) * 0.125
            mv[1, t, here, :] = squares * 0.125
            return 0

        lax.fori_loop(0, 6, finish, 0)
        mine = pl.ds(pl.multiple_of(kept + keep2[half] * 48, 8), 48)
        third[n] = remote(mv.at[:, t, mine, :], mv.at[:, t, mine, :], s3.at[n], q3.at[n], two[half])
        third[n].start()

    fourth = {}
    for t, half in flows:
        n = 2 * t + half
        third[n].wait_recv()
        kept = pl.ds(rows_of(half, keep1[half]), 96)
        fourth[n] = remote(mv.at[:, t, kept, :], mv.at[:, t, kept, :], s4.at[n], q4.at[n], one[half])
        fourth[n].start()

    outs = []
    for t in range(3):
        for half in range(2):
            fourth[2 * t + half].wait_recv()
        part = pl.ds(128 * t, 128)
        for number, target in enumerate((mean_ref, var_ref)):
            copy = pltpu.make_async_copy(mv.at[number, t], target.at[0, :, part], osem.at[number, t])
            copy.start()
            outs.append(copy)
    for n in range(6):
        first[n].wait_send()
        second[n].wait_send()
        third[n].wait_send()
        fourth[n].wait_send()
    for copy in outs:
        copy.wait()


def reduce_members(peak):
    shape = jax.ShapeDtypeStruct((1, 384, 384), jnp.float32)
    sems = [pltpu.SemaphoreType.DMA((6,))] * 8
    return pl.pallas_call(
        reduce_kernel,
        out_shape=(shape, shape),
        in_specs=[vmem_spec()],
        out_specs=(any_spec(), any_spec()),
        scratch_shapes=[
            VMEM((6, 2, 96, 128), jnp.float32),
            VMEM((6, 2, 96, 128), jnp.float32),
            VMEM((6, 2, 48, 128), jnp.float32),
            VMEM((2, 3, 384, 128), jnp.float32),
            *sems,
            pltpu.SemaphoreType.DMA((2, 3)),
        ],
        compiler_params=pltpu.CompilerParams(
            collective_id=2, has_side_effects=True, vmem_limit_bytes=40 << 20
        ),
        name="reduce",
    )(peak)


def body(outer_source, outer_depth, wet_tiles, nest_host, nest_anchor, nest_source, nest_depth):
    eta = outer_source.reshape(2, 16, 8, 1024)
    depth = outer_depth.reshape(16, 8, 1024)
    halos = exchange_halos(eta, depth)
    level, flux, edges, pick = outer_steps(wet_tiles, nest_host, nest_anchor, eta, depth, halos)
    own = route_edges(nest_host, pick, edges)
    peak = advance_nests(own, nest_source, nest_depth)
    mean, var = reduce_members(peak)
    return (level.reshape(2, 128, 1024), flux.reshape(2, 2, 128, 1024), mean, var)


def solution(mesh):
    return jax.shard_map(
        body,
        mesh=mesh,
        in_specs=(
            P("mem", "sec", None),
            P("sec", None),
            P(),
            P(),
            P(),
            P("mem", "sec", None, None),
            P("sec", None, None),
        ),
        out_specs=(
            P("mem", "sec", None),
            P(None, "mem", "sec", None),
            P("sec", None, None),
            P("sec", None, None),
        ),
        check_vma=False,
    )
```

time: 537 us -> 145 us (0.27)
  local copies, waits for them, and re-layouts: 172 us -> 8.42 us
  Pallas kernels: 0 us -> 135 us
  blocking collectives: 135 us -> 0 us
  other arithmetic: 90.5 us -> 0 us
  waiting for transfers between devices: 88.8 us -> 0 us
  between operations: 24.9 us -> 0.78 us
  starting transfers between devices: 18.8 us -> 0 us
    pallas_call x0 -> x5, Pallas kernels: none -> 135 us  [the longest x1 69.8 us: advance_nests(): pl.pallas_call(nest_kernel, out_shape=jax.ShapeDtypeStruct((2, 3, 384, 12...]
    all_gather x3 -> x0, blocking collectives: 135 us -> none  [body(): gathered = lax.all_gather(host_slots(surface), 'sec', axis=0, tiled=True)]
    broadcast_in_dim x145 -> x0, local copies, waits for them, and re-layouts: 122 us -> none  [the longest x18 17.5 us: force_edges(): updated = jnp.where(row_ids == 0, top_edge, updated)]
    psum x2 -> x0, waiting for transfers between devices: 84.9 us -> none  [the longest x1 45.2 us: body(): member_total = lax.psum(jnp.sum(peak_level, axis=0), 'mem')]
    max x18 -> x0, other arithmetic: 48 us -> none  [one_substep(): return (fine_level, fine_x, fine_y, jnp.maximum(peak_level, fine_level))]
    while x132 -> x0, local copies, waits for them, and re-layouts: 28 us -> none
    ppermute x6 -> x0, starting transfers between devices: 18.7 us -> none  [passed_along(): lax.ppermute(value, axis, [(source, source + steps) for source in range(i...]
    slice x72 -> x0, local copies, waits for them, and re-layouts: 17.1 us -> none  [the longest x21 7.64 us: from_right(): field[..., 1:]]
  transfers between devices with their start and end apart: 8 -> 0, of which waited for: 4 -> 0; matrix products, arithmetic and copies ran while one was open for 13% -> 0% of each run, Pallas kernels for 0% -> 0%
where the time goes in v1:
time: 145 us; the launch traced here: 144 us
  Pallas kernels  135 us (93%)
  local copies, waits for them, and re-layouts  8.42 us (6%)
    pallas_call x1, Pallas kernels, advance_nests(): pl.pallas_call(nest_kernel, out_shape=jax.ShapeDtypeStruct((2, 3, 384, 12...  69.8 us
    pallas_call x1, Pallas kernels, reduce_members(): pl.pallas_call(reduce_kernel, out_shape=(shape, shape), in_specs=[vmem_sp...  24.5 us
    pallas_call x1, Pallas kernels, route_edges(): pl.pallas_call(route_kernel, out_shape=jax.ShapeDtypeStruct((16, 128), jn...  15.6 us
    pallas_call x1, Pallas kernels, outer_steps(): pl.pallas_call(outer_kernel, out_shape=(jax.ShapeDtypeStruct((2, 16, 8, 1...  14.7 us
    pallas_call x1, Pallas kernels, exchange_halos(): pl.pallas_call(halo_kernel, out_shape=(rows, rows, coef, coef), in_specs=...  10.3 us
    unnamed x28, local copies, waits for them, and re-layouts  8.42 us

profile of v1, /device:TPU:1, one launch (start us, length us, event | category | flops | bytes accessed | tf_op | source)
XLA Modules:
  0.0 144.2 jit_solution(12970578809578728348)
XLA Ops:
  0.6 0.0 copy-start.10
  0.6 0.0 copy-start.1
  0.7 0.0 copy-start
  0.7 0.9 copy.11.wet_ref
  1.6 0.8 copy.12.anchor_ref
  2.3 10.3 %halo.1 = (f32[2,8,1024]{2,1,0:T(8,128)}, f32[2,8,1024]{2,1,0:T(8,128)}, f32[8,1024]{1,0:T(8,128)}, f32[8,1024]{1,0:T(8,128)}) custom-call(f32[2,16,8,1024]{3,2,1,0:T(8,128)} %bitcast.4, f32[16,8,1024]{2,1,0:T(8,128)} %bitcast.6), custom_call_target="tpu_custom_call" | custom-call | tf_op jit(solution)/shard_map/halo/pallas_call | solution.py:64
  12.7 0.0 copy-start.2
  12.7 0.0 copy-start.3
  12.7 0.0 copy-done.10
  12.7 0.0 copy-done.1
  12.7 0.0 copy-done
  12.7 0.0 copy-start.4
  12.7 1.0 copy-done.4
  13.7 0.0 copy-start.5
  13.7 0.8 copy-done.5
  14.5 0.0 copy-start.6
  14.5 0.8 copy-done.6
  15.3 0.0 copy-start.7
  15.3 0.8 copy-done.7
  16.0 14.7 %outer.1 = (f32[2,16,8,1024]{3,2,1,0:T(8,128)}, f32[2,2,16,8,1024]{4,3,2,1,0:T(8,128)}, f32[2,16,128]{2,1,0:T(8,128)S(1)}, s32[64]{0:T(128)S(1)}) custom-call(s32[64,8]{1,0:T(8,128)S(1)} %copy.11.wet_ref, s32[64]{0:T(128)S(1)} %copy-done.10, s32[64,2]{1,0:T(8,128)S(1)} %copy.12.anchor_ref, f32[2,16,8,1024]{3,2,1,0:T(8,128)S(1)} %bitcast.5, ...), custom_call_target="tpu_custom_call" | custom-call | tf_op jit(solution)/shard_map/outer/pallas_call | solution.py:234
  30.7 0.0 copy-start.9
  30.7 0.6 copy-done.9
  31.3 0.5 copy-done.11
  31.8 15.6 %route.1.edge_ref = f32[16,128]{1,0:T(8,128)} custom-call(s32[64]{0:T(128)} %host_ref.3, s32[64]{0:T(128)} %copy-done.11, f32[2,16,128]{2,1,0:T(8,128)} %copy-done.9), custom_call_target="tpu_custom_call" | custom-call | tf_op jit(solution)/shard_map/route/pallas_call | solution.py:316
  47.5 0.0 copy-done.2
  47.5 0.0 copy-done.3
  47.5 0.0 copy-start.8
  47.5 0.7 copy-done.8
  48.2 69.8 %nests.1.peak_ref = f32[2,3,384,128]{3,2,1,0:T(8,128)S(1)} custom-call(f32[16,128]{1,0:T(8,128)S(1)} %copy-done.8, f32[2,1,384,384]{3,2,1,0:T(8,128)S(1)} %copy-done.2, f32[1,384,384]{2,1,0:T(8,128)S(1)} %copy-done.3), custom_call_target="tpu_custom_call" | custom-call | tf_op jit(solution)/shard_map/nests/pallas_call | solution.py:455
  118.0 24.5 %reduce.1 = (f32[1,384,384]{2,1,0:T(8,128)S(1)}, f32[1,384,384]{2,1,0:T(8,128)S(1)}) custom-call(f32[2,3,384,128]{3,2,1,0:T(8,128)S(1)} %nests.1.peak_ref), custom_call_target="tpu_custom_call" | custom-call | tf_op jit(solution)/shard_map/reduce/pallas_call | solution.py:592
  142.5 0.8 copy.15
  143.4 0.8 copy.16
  (1 shorter events, 0.0 us)
Async XLA Ops:
  0.6 12.1 %copy-start.10 = (s32[64]{0:T(128)S(1)}, s32[64]{0:T(128)}, u32[]{:S(2)}) copy-start(s32[64]{0:T(128)} %host_ref.3) | copy-start | bytes 772
  0.6 12.1 %copy-start.1 = (f32[128,1024]{1,0:T(8,128)S(1)}, f32[128,1024]{1,0:T(8,128)}, u32[]{:S(2)}) copy-start(f32[128,1024]{1,0:T(8,128)} %param.8) | copy-start | bytes 1572868
  0.7 12.1 %copy-start = (f32[2,128,1024]{2,1,0:T(8,128)S(1)}, f32[2,128,1024]{2,1,0:T(8,128)}, u32[]{:S(2)}) copy-start(f32[2,128,1024]{2,1,0:T(8,128)} %param.7) | copy-start | bytes 3145732
  12.7 34.8 %copy-start.2 = (f32[2,1,384,384]{3,2,1,0:T(8,128)S(1)}, f32[2,1,384,384]{3,2,1,0:T(8,128)}, u32[]{:S(2)}) copy-start(f32[2,1,384,384]{3,2,1,0:T(8,128)} %source_ref.1) | copy-start | bytes 3538948
  12.7 34.8 %copy-start.3 = (f32[1,384,384]{2,1,0:T(8,128)S(1)}, f32[1,384,384]{2,1,0:T(8,128)}, u32[]{:S(2)}) copy-start(f32[1,384,384]{2,1,0:T(8,128)} %depth_ref.1) | copy-start | bytes 1769476
  12.7 1.0 copy-start.4
  13.7 0.8 copy-start.5
  14.5 0.8 copy-start.6
  15.3 0.8 copy-start.7
  30.7 0.6 copy-start.9
  31.3 0.5 copy-start.11
  47.5 0.7 copy-start.8

commit v2 on v1

--- a/solution.py
+++ b/solution.py
@@ -12,6 +12,7 @@
 X_PLANES = 4
 Z_CORES = 16
 STRIP = 48
+BATCH = 48
 VMEM = pltpu.VMEM
 ANY = pl.ANY
 
@@ -332,26 +333,47 @@
     )(nest_host, pick, edges)
 
 
-def nest_kernel(edge_ref, source_ref, depth_ref, peak_ref, h, div, peak, coef, cols, rows, src, dsrc, sem):
-    copies = []
+def lane_ids():
+    return lax.broadcasted_iota(jnp.int32, (8, 128), 1)
+
+
+def sub_ids():
+    return lax.broadcasted_iota(jnp.int32, (8, 128), 0)
+
+
+def interleave(parts):
+    lane = lane_ids()
+    out = []
     for t in range(3):
-        part = pl.ds(128 * t, 128)
-        for m in range(2):
-            copies.append(
-                pltpu.make_async_copy(source_ref.at[m, 0, :, part], src.at[m, t], sem.at[3 * m + t])
-            )
-        copies.append(pltpu.make_async_copy(depth_ref.at[0, :, part], dsrc.at[t], sem.at[6 + t]))
-    for copy in copies:
-        copy.start()
-
-    lane = lax.broadcasted_iota(jnp.int32, (8, 128), 1)
-    sub = lax.broadcasted_iota(jnp.int32, (8, 128), 0)
+        origin = (3 * lax.rem((lane - t + 128) * 43, 128) + t) // 128
+        mixed = jnp.where(origin == 0, parts[0], jnp.where(origin == 1, parts[1], parts[2]))
+        out.append(jnp.take_along_axis(mixed, lax.rem(3 * lane + t, 128), axis=1))
+    return out
+
+
+def straighten(parts):
+    lane = lane_ids()
+    spread_parts = []
+    origins = []
+    for t in range(3):
+        spot = lax.rem((lane - t + 128) * 43, 128)
+        spread_parts.append(jnp.take_along_axis(parts[t], spot, axis=1))
+        origins.append((3 * spot + t) // 128)
+    return [
+        jnp.where(origins[0] == t, spread_parts[0], jnp.where(origins[1] == t, spread_parts[1], spread_parts[2]))
+        for t in range(3)
+    ]
+
+
+def spread_edges(edge_ref, cols, rows, steps):
+    lane = lane_ids()
+    sub = sub_ids()
 
     def spread(row, index):
         wide = jnp.broadcast_to(row, (8, 128))
         return jnp.take_along_axis(wide, index, axis=1)
 
-    for step in range(STEPS):
+    for step in steps:
         for m in range(2):
             at = (step * 2 + m) * 2
             level = edge_ref[at : at + 1, :]
@@ -361,94 +383,139 @@
                 cols[step, m, 1, q] = spread(upright, sub * 8 + q + 64)
             for side in range(2):
                 for t in range(3):
-                    value = spread(level, (lane + 128 * t) // REFINE + 64 * side)
+                    value = spread(level, (3 * lane + t) // REFINE + 64 * side)
                     if t == 0:
                         value = jnp.where(lane == 0, cols[step, m, 0, 7 * side], value)
                     if t == 2:
                         value = jnp.where(lane == 127, cols[step, m, 1, 7 * side], value)
                     rows[step, m, side, t] = value
 
-    def force(value, step, m, t, i, side):
-        if side is not None:
-            edge_sub = 0 if side == 0 else 7
-            value = jnp.where(sub == edge_sub, rows[step, m, side, t], value)
-        if t == 0:
-            value = jnp.where(lane == 0, cols[step, m, 0, i // REFINE], value)
-        if t == 2:
-            value = jnp.where(lane == 127, cols[step, m, 1, i // REFINE], value)
-        return value
-
+
+def force_sides(value, t, sides):
+    lane = lane_ids()
+    if t == 0:
+        value = jnp.where(lane == 0, sides[0], value)
+    if t == 2:
+        value = jnp.where(lane == 127, sides[1], value)
+    return value
+
+
+def fix_rows(h, rows, step, m):
+    sub = sub_ids()
+    for t in range(3):
+        h[m, 0, t] = jnp.where(sub == 0, rows[step, m, 0, t], h[m, 0, t])
+        h[m, STRIP - 1, t] = jnp.where(sub == 7, rows[step, m, 1, t], h[m, STRIP - 1, t])
+
+
+def load_depth(dsrc, coef, d2):
+    def load(i, _):
+        parts = interleave([dsrc[t, pl.ds(i, 8, stride=STRIP), :] for t in range(3)])
+        for t in range(3):
+            coef[i, t] = parts[t]
+        d2[i] = pltpu.roll(parts[2], 1, 1)
+        return 0
+
+    lax.fori_loop(0, STRIP, load, 0, unroll=4)
+
+
+def load_source(src, h, div, peak, cols, rows, m):
+    def load(i, _):
+        parts = interleave([src[m, t, pl.ds(i, 8, stride=STRIP), :] for t in range(3)])
+        sides = [cols[0, m, side, i // REFINE] for side in range(2)]
+        for t in range(3):
+            value = force_sides(parts[t], t, sides)
+            h[m, i, t] = value
+            peak[m, i, t] = value
+            div[m, i, t] = jnp.zeros((8, 128), jnp.float32)
+        return 0
+
+    lax.fori_loop(0, STRIP, load, 0, unroll=4)
+    fix_rows(h, rows, 0, m)
+
+
+def advance(m, start, step, carry, h, div, peak, coef, d2, cols):
+    now, above = carry
+    for r in range(BATCH):
+        i = start + r
+        if r % REFINE == 0:
+            sides = [cols[step, m, side, i // REFINE] for side in range(2)]
+        following = [h[m, i + 1, t] for t in range(3)]
+        d = [coef[i, t] for t in range(3)]
+        beyond = [now[1], now[2], pltpu.roll(now[0], 127, 1)]
+        f = [d[t] * (beyond[t] - now[t]) for t in range(3)]
+        behind = [d2[i] * (now[0] - pltpu.roll(now[2], 1, 1)), f[0], f[1]]
+        g = []
+        for t in range(3):
+            g.append(d[t] * (following[t] - now[t]))
+            change = div[m, i, t] - ((f[t] - behind[t]) + (g[t] - above[t]))
+            value = force_sides(now[t] - change, t, sides)
+            div[m, i, t] = change
+            h[m, i, t] = value
+            peak[m, i, t] = jnp.maximum(peak[m, i, t], value)
+        now, above = following, g
+    return now, above
+
+
+def substeps(m, low, high, h, div, peak, coef, d2, cols, rows):
+    def substep(k, _):
+        step = k // REFINE
+        now = [h[m, 0, t] for t in range(3)]
+        above = []
+        for t in range(3):
+            wrapped = pltpu.roll(now[t], 7, 0)
+            h[m, STRIP, t] = wrapped
+            above.append(pltpu.roll(coef[STRIP - 1, t] * (wrapped - h[m, STRIP - 1, t]), 1, 0))
+        lax.fori_loop(
+            0,
+            STRIP // BATCH,
+            lambda b, c: advance(m, b * BATCH, step, c, h, div, peak, coef, d2, cols),
+            (now, above),
+        )
+        fix_rows(h, rows, step, m)
+        return 0
+
+    lax.fori_loop(low, high, substep, 0)
+
+
+def store_peak(peak, peak_ref, rows, m):
+    sub = sub_ids()
+    for t in range(3):
+        for side, i, edge_sub in ((0, 0, 0), (1, STRIP - 1, 7)):
+            top = jnp.maximum(
+                jnp.maximum(rows[0, m, side, t], rows[1, m, side, t]), rows[2, m, side, t]
+            )
+            peak[m, i, t] = jnp.where(sub == edge_sub, top, peak[m, i, t])
+
+    def store(i, _):
+        parts = straighten([peak[m, i, t] for t in range(3)])
+        for t in range(3):
+            peak_ref[m, t, pl.ds(i, 8, stride=STRIP), :] = parts[t]
+        return 0
+
+    lax.fori_loop(0, STRIP, store, 0, unroll=4)
+
+
+def nest_kernel(
+    edge_ref, source_ref, depth_ref, peak_ref, h, div, peak, coef, d2, cols, rows, src, dsrc, sem
+):
+    copies = []
+    for t in range(3):
+        part = pl.ds(128 * t, 128)
+        copies.append(pltpu.make_async_copy(depth_ref.at[0, :, part], dsrc.at[t], sem.at[6 + t]))
+        for m in range(2):
+            copies.append(
+                pltpu.make_async_copy(source_ref.at[m, 0, :, part], src.at[m, t], sem.at[3 * m + t])
+            )
+    for copy in copies:
+        copy.start()
+    spread_edges(edge_ref, cols, rows, range(STEPS))
     for copy in copies:
         copy.wait()
-
-    def load(i, side=None):
-        for t in range(3):
-            coef[i, t] = dsrc[t, pl.ds(i, 8, stride=STRIP), :]
-            for m in range(2):
-                value = force(src[m, t, pl.ds(i, 8, stride=STRIP), :], 0, m, t, i, side)
-                h[m, i, t] = value
-                peak[m, i, t] = value
-                div[m, i, t] = jnp.zeros((8, 128), jnp.float32)
-
-    load(0, 0)
-
-    def load_body(i, _):
-        load(i)
-        return 0
-
-    lax.fori_loop(1, STRIP - 1, load_body, 0)
-    load(STRIP - 1, 1)
-
-    def advance(i, step, carry, side=None, last=False):
-        out = []
-        for m in range(2):
-            now, above = carry[m]
-            following = [h[m, i + 1, t] for t in range(3)]
-            lefts = [pltpu.roll(now[t], 127, 1) for t in range(3)]
-            f = []
-            for t in range(3):
-                ahead = lefts[t] if t == 2 else jnp.where(lane == 127, lefts[t + 1], lefts[t])
-                f.append(coef[i, t] * (ahead - now[t]))
-            rights = [pltpu.roll(f[t], 1, 1) for t in range(3)]
-            g = []
-            for t in range(3):
-                behind = rights[t] if t == 0 else jnp.where(lane == 0, rights[t - 1], rights[t])
-                g.append(coef[i, t] * (following[t] - now[t]))
-                change = div[m, i, t] - ((f[t] - behind) + (g[t] - above[t]))
-                value = force(now[t] - change, step, m, t, i, side)
-                div[m, i, t] = change
-                h[m, i, t] = value
-                peak[m, i, t] = jnp.maximum(peak[m, i, t], value)
-            out.append((following, g))
-        return out
-
-    def substep(k, _):
-        step = k // REFINE
-        carry = []
-        for m in range(2):
-            now = [h[m, 0, t] for t in range(3)]
-            above = []
-            for t in range(3):
-                wrapped = pltpu.roll(now[t], 7, 0)
-                h[m, STRIP, t] = wrapped
-                above.append(
-                    pltpu.roll(coef[STRIP - 1, t] * (wrapped - h[m, STRIP - 1, t]), 1, 0)
-                )
-            carry.append((now, above))
-        carry = advance(0, step, carry, side=0)
-        carry = lax.fori_loop(1, STRIP - 1, lambda i, c: advance(i, step, c), carry, unroll=2)
-        advance(STRIP - 1, step, carry, side=1)
-        return 0
-
-    lax.fori_loop(1, STEPS * REFINE, substep, 0)
-
-    def store(i, _):
-        for m in range(2):
-            for t in range(3):
-                peak_ref[m, t, pl.ds(i, 8, stride=STRIP), :] = peak[m, i, t]
-        return 0
-
-    lax.fori_loop(0, STRIP, store, 0)
+    load_depth(dsrc, coef, d2)
+    for m in range(2):
+        load_source(src, h, div, peak, cols, rows, m)
+        substeps(m, 1, STEPS * REFINE, h, div, peak, coef, d2, cols, rows)
+        store_peak(peak, peak_ref, rows, m)
 
 
 def advance_nests(edges, source, depth):
@@ -462,6 +529,7 @@
             VMEM((2, STRIP, 3, 8, 128), jnp.float32),
             VMEM((2, STRIP, 3, 8, 128), jnp.float32),
             VMEM((STRIP, 3, 8, 128), jnp.float32),
+            VMEM((STRIP, 8, 128), jnp.float32),
             VMEM((STEPS, 2, 2, 8, 8, 128), jnp.float32),
             VMEM((STEPS, 2, 2, 3, 8, 128), jnp.float32),
             VMEM((2, 3, 384, 128), jnp.float32),

time: 145 us -> 91 us (0.63)
  Pallas kernels: 135 us -> 81.4 us
    pallas_call x1, Pallas kernels: 69.8 us -> 16.3 us  [advance_nests(): pl.pallas_call(nest_kernel, out_shape=jax.ShapeDtypeStruct((2, 3, 384, 12...]
where the time goes in v2:
time: 91 us; the launch traced here: 90.6 us
  Pallas kernels  81.4 us (89%)
  local copies, waits for them, and re-layouts  8.42 us (9%)
    pallas_call x1, Pallas kernels, reduce_members(): pl.pallas_call(reduce_kernel, out_shape=(shape, shape), in_specs=[vmem_sp...  24.5 us
    pallas_call x1, Pallas kernels, advance_nests(): pl.pallas_call(nest_kernel, out_shape=jax.ShapeDtypeStruct((2, 3, 384, 12...  16.3 us
    pallas_call x1, Pallas kernels, route_edges(): pl.pallas_call(route_kernel, out_shape=jax.ShapeDtypeStruct((16, 128), jn...  15.6 us
    pallas_call x1, Pallas kernels, outer_steps(): pl.pallas_call(outer_kernel, out_shape=(jax.ShapeDtypeStruct((2, 16, 8, 1...  14.7 us
    pallas_call x1, Pallas kernels, exchange_halos(): pl.pallas_call(halo_kernel, out_shape=(rows, rows, coef, coef), in_specs=...  10.3 us
    unnamed x28, local copies, waits for them, and re-layouts  8.42 us

profile of v2, /device:TPU:1, one launch (start us, length us, event | category | flops | bytes accessed | tf_op | source)
XLA Modules:
  0.0 90.6 jit_solution(3317998768696487392)
XLA Ops:
  0.6 0.0 copy-start.10
  0.6 0.0 copy-start.1
  0.7 0.0 copy-start
  0.7 0.9 copy.11.wet_ref
  1.6 0.8 copy.12.anchor_ref
  2.3 10.3 %halo.1 = (f32[2,8,1024]{2,1,0:T(8,128)}, f32[2,8,1024]{2,1,0:T(8,128)}, f32[8,1024]{1,0:T(8,128)}, f32[8,1024]{1,0:T(8,128)}) custom-call(f32[2,16,8,1024]{3,2,1,0:T(8,128)} %bitcast.4, f32[16,8,1024]{2,1,0:T(8,128)} %bitcast.6), custom_call_target="tpu_custom_call" | custom-call | tf_op jit(solution)/shard_map/halo/pallas_call | solution.py:65
  12.7 0.0 copy-start.2
  12.7 0.0 copy-start.3
  12.7 0.0 copy-done.10
  12.7 0.0 copy-done.1
  12.7 0.0 copy-done
  12.7 0.0 copy-start.4
  12.7 1.0 %copy-done.4 = f32[2,8,1024]{2,1,0:T(8,128)S(1)} copy-done((f32[2,8,1024]{2,1,0:T(8,128)S(1)}, f32[2,8,1024]{2,1,0:T(8,128)}, u32[]{:S(2)}) %copy-start.4) | copy-done | bytes 65560
  13.7 0.0 copy-start.5
  13.7 0.8 copy-done.5
  14.5 0.0 copy-start.6
  14.5 0.8 copy-done.6
  15.3 0.0 copy-start.7
  15.3 0.8 copy-done.7
  16.0 14.7 %outer.1 = (f32[2,16,8,1024]{3,2,1,0:T(8,128)}, f32[2,2,16,8,1024]{4,3,2,1,0:T(8,128)}, f32[2,16,128]{2,1,0:T(8,128)S(1)}, s32[64]{0:T(128)S(1)}) custom-call(s32[64,8]{1,0:T(8,128)S(1)} %copy.11.wet_ref, s32[64]{0:T(128)S(1)} %copy-done.10, s32[64,2]{1,0:T(8,128)S(1)} %copy.12.anchor_ref, f32[2,16,8,1024]{3,2,1,0:T(8,128)S(1)} %bitcast.5, ...), custom_call_target="tpu_custom_call" | custom-call | tf_op jit(solution)/shard_map/outer/pallas_call | solution.py:235
  30.7 0.0 copy-start.9
  30.7 0.6 copy-done.9
  31.3 0.5 copy-done.11
  31.8 15.6 %route.1.edge_ref = f32[16,128]{1,0:T(8,128)} custom-call(s32[64]{0:T(128)} %host_ref.3, s32[64]{0:T(128)} %copy-done.11, f32[2,16,128]{2,1,0:T(8,128)} %copy-done.9), custom_call_target="tpu_custom_call" | custom-call | tf_op jit(solution)/shard_map/route/pallas_call | solution.py:317
  47.5 0.0 copy-done.2
  47.5 0.0 copy-done.3
  47.5 0.0 copy-start.8
  47.5 0.7 copy-done.8
  48.2 16.3 %nests.1.peak_ref = f32[2,3,384,128]{3,2,1,0:T(8,128)S(1)} custom-call(f32[16,128]{1,0:T(8,128)S(1)} %copy-done.8, f32[2,1,384,384]{3,2,1,0:T(8,128)S(1)} %copy-done.2, f32[1,384,384]{2,1,0:T(8,128)S(1)} %copy-done.3), custom_call_target="tpu_custom_call" | custom-call | tf_op jit(solution)/shard_map/nests/pallas_call | solution.py:522
  64.5 24.5 %reduce.1 = (f32[1,384,384]{2,1,0:T(8,128)S(1)}, f32[1,384,384]{2,1,0:T(8,128)S(1)}) custom-call(f32[2,3,384,128]{3,2,1,0:T(8,128)S(1)} %nests.1.peak_ref), custom_call_target="tpu_custom_call" | custom-call | tf_op jit(solution)/shard_map/reduce/pallas_call | solution.py:660
  89.0 0.8 copy.15
  89.8 0.8 copy.16
  (1 shorter events, 0.0 us)
Async XLA Ops:
  0.6 12.1 %copy-start.10 = (s32[64]{0:T(128)S(1)}, s32[64]{0:T(128)}, u32[]{:S(2)}) copy-start(s32[64]{0:T(128)} %host_ref.3) | copy-start | bytes 772
  0.6 12.1 %copy-start.1 = (f32[128,1024]{1,0:T(8,128)S(1)}, f32[128,1024]{1,0:T(8,128)}, u32[]{:S(2)}) copy-start(f32[128,1024]{1,0:T(8,128)} %param.8) | copy-start | bytes 1572868
  0.7 12.1 %copy-start = (f32[2,128,1024]{2,1,0:T(8,128)S(1)}, f32[2,128,1024]{2,1,0:T(8,128)}, u32[]{:S(2)}) copy-start(f32[2,128,1024]{2,1,0:T(8,128)} %param.7) | copy-start | bytes 3145732
  12.7 34.8 %copy-start.2 = (f32[2,1,384,384]{3,2,1,0:T(8,128)S(1)}, f32[2,1,384,384]{3,2,1,0:T(8,128)}, u32[]{:S(2)}) copy-start(f32[2,1,384,384]{3,2,1,0:T(8,128)} %source_ref.1) | copy-start | bytes 3538948
  12.7 34.8 %copy-start.3 = (f32[1,384,384]{2,1,0:T(8,128)S(1)}, f32[1,384,384]{2,1,0:T(8,128)}, u32[]{:S(2)}) copy-start(f32[1,384,384]{2,1,0:T(8,128)} %depth_ref.1) | copy-start | bytes 1769476
  12.7 1.0 %copy-start.4 = (f32[2,8,1024]{2,1,0:T(8,128)S(1)}, f32[2,8,1024]{2,1,0:T(8,128)}, u32[]{:S(2)}) copy-start(f32[2,8,1024]{2,1,0:T(8,128)} %get-tuple-element.14.up_eta) | copy-start | bytes 196612
  13.7 0.8 copy-start.5
  14.5 0.8 copy-start.6
  15.3 0.8 copy-start.7
  30.7 0.6 copy-start.9
  31.3 0.5 copy-start.11
  47.5 0.7 copy-start.8

commit v3 on v2

--- a/solution.py
+++ b/solution.py
@@ -256,83 +256,6 @@
     )(wet_tiles, nest_host, nest_anchor, eta, depth, *halos)
 
 
-def route_kernel(
-    host_ref, pick_ref, edges_ref, out_ref,
-    gathered, outgoing, incoming, send_x, recv_x, send_z, recv_z,
-):
-    me = lax.axis_index("sec")
-    plane = me // Z_CORES
-    spot = lax.rem(me, Z_CORES)
-    barrier = pltpu.get_barrier_semaphore()
-    for step in range(1, X_PLANES):
-        peer = lax.rem(plane + step, X_PLANES) * Z_CORES + spot
-        pl.semaphore_signal(barrier, inc=1, device_id={"sec": peer}, device_id_type=MESH)
-    for step in range(1, Z_CORES):
-        peer = plane * Z_CORES + lax.rem(spot + step, Z_CORES)
-        pl.semaphore_signal(barrier, inc=1, device_id={"sec": peer}, device_id_type=MESH)
-    gathered[plane] = edges_ref[...]
-    pl.semaphore_wait(barrier, X_PLANES + Z_CORES - 2)
-
-    copies = []
-    for step in range(1, X_PLANES):
-        peer = lax.rem(plane + step, X_PLANES) * Z_CORES + spot
-        copy = pltpu.make_async_remote_copy(
-            src_ref=edges_ref,
-            dst_ref=gathered.at[plane],
-            send_sem=send_x.at[step - 1],
-            recv_sem=recv_x.at[step - 1],
-            device_id={"sec": peer},
-            device_id_type=MESH,
-        )
-        copy.start()
-        copies.append(copy)
-    for copy in copies:
-        copy.wait()
-
-    second = []
-    for step in range(Z_CORES):
-        target = lax.rem(spot + step, Z_CORES)
-        choice = pick_ref[plane * Z_CORES + target]
-        message = gathered[choice // 2, lax.rem(choice, 2)]
-        if step == 0:
-            incoming[spot] = message
-            continue
-        outgoing[step] = message
-        copy = pltpu.make_async_remote_copy(
-            src_ref=outgoing.at[step],
-            dst_ref=incoming.at[spot],
-            send_sem=send_z.at[step - 1],
-            recv_sem=recv_z.at[step - 1],
-            device_id={"sec": plane * Z_CORES + target},
-            device_id_type=MESH,
-        )
-        copy.start()
-        second.append(copy)
-    for copy in second:
-        copy.wait()
-    out_ref[...] = incoming[lax.rem(host_ref[me], Z_CORES)]
-
-
-def route_edges(nest_host, pick, edges):
-    return pl.pallas_call(
-        route_kernel,
-        out_shape=jax.ShapeDtypeStruct((16, 128), jnp.float32),
-        in_specs=[smem_spec(), smem_spec(), vmem_spec()],
-        out_specs=vmem_spec(),
-        scratch_shapes=[
-            VMEM((X_PLANES, 2, 16, 128), jnp.float32),
-            VMEM((Z_CORES, 16, 128), jnp.float32),
-            VMEM((Z_CORES, 16, 128), jnp.float32),
-            pltpu.SemaphoreType.DMA((X_PLANES - 1,)),
-            pltpu.SemaphoreType.DMA((X_PLANES - 1,)),
-            pltpu.SemaphoreType.DMA((Z_CORES - 1,)),
-            pltpu.SemaphoreType.DMA((Z_CORES - 1,)),
-        ],
-        compiler_params=pltpu.CompilerParams(collective_id=1, has_side_effects=True),
-        name="route",
-    )(nest_host, pick, edges)
-
-
 def lane_ids():
     return lax.broadcasted_iota(jnp.int32, (8, 128), 1)
 
@@ -418,18 +341,30 @@
     lax.fori_loop(0, STRIP, load, 0, unroll=4)
 
 
-def load_source(src, h, div, peak, cols, rows, m):
+def load_source(src, h, div, m):
     def load(i, _):
         parts = interleave([src[m, t, pl.ds(i, 8, stride=STRIP), :] for t in range(3)])
-        sides = [cols[0, m, side, i // REFINE] for side in range(2)]
         for t in range(3):
-            value = force_sides(parts[t], t, sides)
-            h[m, i, t] = value
-            peak[m, i, t] = value
+            h[m, i, t] = parts[t]
             div[m, i, t] = jnp.zeros((8, 128), jnp.float32)
         return 0
 
     lax.fori_loop(0, STRIP, load, 0, unroll=4)
+
+
+def first_substep(h, peak, cols, rows, m):
+    def start(q, _):
+        sides = [cols[0, m, side, q] for side in range(2)]
+        for r in range(REFINE):
+            for t in range(3):
+                i = q * REFINE + r
+                value = force_sides(h[m, i, t], t, sides)
+                if t != 1:
+                    h[m, i, t] = value
+                peak[m, i, t] = value
+        return 0
+
+    lax.fori_loop(0, STRIP // REFINE, start, 0)
     fix_rows(h, rows, 0, m)
 
 
@@ -495,109 +430,144 @@
     lax.fori_loop(0, STRIP, store, 0, unroll=4)
 
 
-def nest_kernel(
-    edge_ref, source_ref, depth_ref, peak_ref, h, div, peak, coef, d2, cols, rows, src, dsrc, sem
+def coast_kernel(
+    host_ref, pick_ref, edges_ref, source_ref, depth_ref, mean_ref, var_ref,
+    gathered, outgoing, incoming, own_edge,
+    h, div, peak, coef, d2, cols, rows, src, dsrc, pn,
+    r1, st, r2, mv,
+    load_sem, send_x, recv_x, send_z, recv_z, s1, q1, s2, q2, s3, q3, s4, q4, osem,
 ):
-    copies = []
+    sec = lax.axis_index("sec")
+    plane = sec // Z_CORES
+    spot = lax.rem(sec, Z_CORES)
+    mem = lax.axis_index("mem")
+    near = mem + 1 - 2 * lax.rem(mem, 2)
+    far = 3 - mem
+    high = mem // 2
+    gray = lax.rem(lax.rem(mem, 2) + high, 2)
+
+    loads = []
     for t in range(3):
         part = pl.ds(128 * t, 128)
-        copies.append(pltpu.make_async_copy(depth_ref.at[0, :, part], dsrc.at[t], sem.at[6 + t]))
-        for m in range(2):
-            copies.append(
-                pltpu.make_async_copy(source_ref.at[m, 0, :, part], src.at[m, t], sem.at[3 * m + t])
+        loads.append(pltpu.make_async_copy(depth_ref.at[0, :, part], dsrc.at[t], load_sem.at[t]))
+    for m in range(2):
+        for t in range(3):
+            part = pl.ds(128 * t, 128)
+            loads.append(
+                pltpu.make_async_copy(
+                    source_ref.at[m, 0, :, part], src.at[m, t], load_sem.at[3 + 3 * m + t]
+                )
             )
-    for copy in copies:
+    for copy in loads:
         copy.start()
-    spread_edges(edge_ref, cols, rows, range(STEPS))
-    for copy in copies:
+
+    barrier = pltpu.get_barrier_semaphore()
+    for step in range(1, X_PLANES):
+        peer = lax.rem(plane + step, X_PLANES) * Z_CORES + spot
+        pl.semaphore_signal(barrier, inc=1, device_id={"sec": peer}, device_id_type=MESH)
+    for step in range(1, Z_CORES):
+        peer = plane * Z_CORES + lax.rem(spot + step, Z_CORES)
+        pl.semaphore_signal(barrier, inc=1, device_id={"sec": peer}, device_id_type=MESH)
+    for peer in (near, far):
+        pl.semaphore_signal(barrier, inc=1, device_id={"mem": peer}, device_id_type=MESH)
+    gathered[plane] = edges_ref[...]
+    pl.semaphore_wait(barrier, X_PLANES + Z_CORES)
+
+    along_x = []
+    for step in range(1, X_PLANES):
+        peer = lax.rem(plane + step, X_PLANES) * Z_CORES + spot
+        copy = pltpu.make_async_remote_copy(
+            src_ref=edges_ref,
+            dst_ref=gathered.at[plane],
+            send_sem=send_x.at[step - 1],
+            recv_sem=recv_x.at[step - 1],
+            device_id={"sec": peer},
+            device_id_type=MESH,
+        )
+        copy.start()
+        along_x.append(copy)
+    for copy in loads[:3]:
         copy.wait()
     load_depth(dsrc, coef, d2)
+    for copy in along_x:
+        copy.wait()
+    along_z = []
+    for step in range(Z_CORES):
+        target = lax.rem(spot + step, Z_CORES)
+        choice = pick_ref[plane * Z_CORES + target]
+        message = gathered[choice // 2, lax.rem(choice, 2)]
+        if step == 0:
+            incoming[spot] = message
+            continue
+        outgoing[step] = message
+        copy = pltpu.make_async_remote_copy(
+            src_ref=outgoing.at[step],
+            dst_ref=incoming.at[spot],
+            send_sem=send_z.at[step - 1],
+            recv_sem=recv_z.at[step - 1],
+            device_id={"sec": plane * Z_CORES + target},
+            device_id_type=MESH,
+        )
+        copy.start()
+        along_z.append(copy)
+    for copy in loads[3:]:
+        copy.wait()
     for m in range(2):
-        load_source(src, h, div, peak, cols, rows, m)
-        substeps(m, 1, STEPS * REFINE, h, div, peak, coef, d2, cols, rows)
-        store_peak(peak, peak_ref, rows, m)
-
-
-def advance_nests(edges, source, depth):
-    return pl.pallas_call(
-        nest_kernel,
-        out_shape=jax.ShapeDtypeStruct((2, 3, 384, 128), jnp.float32),
-        in_specs=[vmem_spec(), any_spec(), any_spec()],
-        out_specs=vmem_spec(),
-        scratch_shapes=[
-            VMEM((2, STRIP + 1, 3, 8, 128), jnp.float32),
-            VMEM((2, STRIP, 3, 8, 128), jnp.float32),
-            VMEM((2, STRIP, 3, 8, 128), jnp.float32),
-            VMEM((STRIP, 3, 8, 128), jnp.float32),
-            VMEM((STRIP, 8, 128), jnp.float32),
-            VMEM((STEPS, 2, 2, 8, 8, 128), jnp.float32),
-            VMEM((STEPS, 2, 2, 3, 8, 128), jnp.float32),
-            VMEM((2, 3, 384, 128), jnp.float32),
-            VMEM((3, 384, 128), jnp.float32),
-            pltpu.SemaphoreType.DMA((9,)),
-        ],
-        compiler_params=pltpu.CompilerParams(vmem_limit_bytes=40 << 20),
-        name="nests",
-    )(edges, source, depth)
-
-
-def reduce_kernel(peak_ref, mean_ref, var_ref, r1, st, r2, mv, s1, q1, s2, q2, s3, q3, s4, q4, osem):
-    m = lax.axis_index("mem")
-    near = m + 1 - 2 * lax.rem(m, 2)
-    far = 3 - m
-    high = m // 2
-    gray = lax.rem(lax.rem(m, 2) + high, 2)
-    barrier = pltpu.get_barrier_semaphore()
-    for peer in (near, far):
-        pl.semaphore_signal(barrier, inc=1, device_id={"mem": peer}, device_id_type=MESH)
-    pl.semaphore_wait(barrier, 2)
+        load_source(src, h, div, m)
+    for copy in along_z:
+        copy.wait()
+    own_edge[...] = incoming[lax.rem(host_ref[sec], Z_CORES)]
+    spread_edges(own_edge, cols, rows, range(STEPS))
 
     one = (near, far)
     two = (far, near)
     keep1 = (gray, high)
     keep2 = (high, gray)
+    flows = [(t, half) for t in range(3) for half in range(2)]
 
     def rows_of(half, bit1):
         return pl.multiple_of(half * 192 + bit1 * 96, 8)
 
-    def remote(src, dst, send, recv, peer):
+    def remote(src_ref, dst_ref, send, recv, peer):
         return pltpu.make_async_remote_copy(
-            src_ref=src, dst_ref=dst, send_sem=send, recv_sem=recv,
+            src_ref=src_ref, dst_ref=dst_ref, send_sem=send, recv_sem=recv,
             device_id={"mem": peer}, device_id_type=MESH,
         )
 
-    flows = [(t, half) for t in range(3) for half in range(2)]
     first = {}
-    for t, half in flows:
-        n = 2 * t + half
-        away = pl.ds(rows_of(half, 1 - keep1[half]), 96)
-        first[n] = remote(peak_ref.at[:, t, away, :], r1.at[n], s1.at[n], q1.at[n], one[half])
-        first[n].start()
+    for m in range(2):
+        first_substep(h, peak, cols, rows, m)
+        substeps(m, 1, STEPS * REFINE, h, div, peak, coef, d2, cols, rows)
+        store_peak(peak, pn, rows, m)
+        for t, half in flows:
+            n = 2 * t + half
+            away = pl.ds(rows_of(half, 1 - keep1[half]), 96)
+            first[m, n] = remote(pn.at[m, t, away, :], r1.at[n, m], s1.at[n, m], q1.at[n, m], one[half])
+            first[m, n].start()
 
     second = {}
     for t, half in flows:
         n = 2 * t + half
-        first[n].wait_recv()
+        for m in range(2):
+            first[m, n].wait_recv()
         kept = rows_of(half, keep1[half])
 
-        def merge(index, part, n=n, t=t, kept=kept):
-            local = pl.multiple_of(part * 48 + index * 8, 8)
-            here = pl.ds(pl.multiple_of(kept + local, 8), 8)
-            a = peak_ref[0, t, here, :]
-            b = peak_ref[1, t, here, :]
-            c = r1[n, 0, pl.ds(local, 8), :]
-            d = r1[n, 1, pl.ds(local, 8), :]
-            total = (a + b) + (c + d)
-            middle = total * 0.25
-            a = a - middle
-            b = b - middle
-            c = c - middle
-            d = d - middle
-            st[n, 0, pl.ds(local, 8), :] = total
-            st[n, 1, pl.ds(local, 8), :] = (a * a + b * b) + (c * c + d * d)
-
-        def merge_part(part):
-            lax.fori_loop(0, 6, lambda index, _: (merge(index, part), 0)[1], 0)
+        def merge_part(part, n=n, t=t, kept=kept):
+            for index in range(6):
+                local = pl.multiple_of(part * 48 + index * 8, 8)
+                here = pl.ds(pl.multiple_of(kept + local, 8), 8)
+                a = pn[0, t, here, :]
+                b = pn[1, t, here, :]
+                c = r1[n, 0, pl.ds(local, 8), :]
+                d = r1[n, 1, pl.ds(local, 8), :]
+                total = (a + b) + (c + d)
+                middle = total * 0.25
+                a = a - middle
+                b = b - middle
+                c = c - middle
+                d = d - middle
+                st[n, 0, pl.ds(local, 8), :] = total
+                st[n, 1, pl.ds(local, 8), :] = (a * a + b * b) + (c * c + d * d)
 
         merge_part(1 - keep2[half])
         away = pl.ds(pl.multiple_of((1 - keep2[half]) * 48, 8), 48)
@@ -610,22 +580,18 @@
         n = 2 * t + half
         second[n].wait_recv()
         kept = rows_of(half, keep1[half])
-
-        def finish(index, _, n=n, t=t, kept=kept, half=half):
-            offset = pl.multiple_of(index * 8, 8)
+        for index in range(6):
+            offset = index * 8
             local = pl.multiple_of(keep2[half] * 48 + offset, 8)
-            own = st[n, 0, pl.ds(local, 8), :]
-            other = r2[n, 0, pl.ds(offset, 8), :]
-            gap = own - other
-            squares = (st[n, 1, pl.ds(local, 8), :] + r2[n, 1, pl.ds(offset, 8), :]) + gap * gap * 0.125
+            mine = st[n, 0, pl.ds(local, 8), :]
+            other = r2[n, 0, offset : offset + 8, :]
+            gap = mine - other
+            squares = (st[n, 1, pl.ds(local, 8), :] + r2[n, 1, offset : offset + 8, :]) + gap * gap * 0.125
             here = pl.ds(pl.multiple_of(kept + local, 8), 8)
-            mv[0, t, here, :] = (own + other) * 0.125
+            mv[0, t, here, :] = (mine + other) * 0.125
             mv[1, t, here, :] = squares * 0.125
-            return 0
-
-        lax.fori_loop(0, 6, finish, 0)
-        mine = pl.ds(pl.multiple_of(kept + keep2[half] * 48, 8), 48)
-        third[n] = remote(mv.at[:, t, mine, :], mv.at[:, t, mine, :], s3.at[n], q3.at[n], two[half])
+        block = pl.ds(pl.multiple_of(kept + keep2[half] * 48, 8), 48)
+        third[n] = remote(mv.at[:, t, block, :], mv.at[:, t, block, :], s3.at[n], q3.at[n], two[half])
         third[n].start()
 
     fourth = {}
@@ -646,7 +612,8 @@
             copy.start()
             outs.append(copy)
     for n in range(6):
-        first[n].wait_send()
+        for m in range(2):
+            first[m, n].wait_send()
         second[n].wait_send()
         third[n].wait_send()
         fourth[n].wait_send()
@@ -654,27 +621,48 @@
         copy.wait()
 
 
-def reduce_members(peak):
+def advance_coast(nest_host, pick, edges, source, depth):
     shape = jax.ShapeDtypeStruct((1, 384, 384), jnp.float32)
-    sems = [pltpu.SemaphoreType.DMA((6,))] * 8
+    dma = pltpu.SemaphoreType.DMA
     return pl.pallas_call(
-        reduce_kernel,
+        coast_kernel,
         out_shape=(shape, shape),
-        in_specs=[vmem_spec()],
+        in_specs=[smem_spec(), smem_spec(), vmem_spec(), any_spec(), any_spec()],
         out_specs=(any_spec(), any_spec()),
         scratch_shapes=[
+            VMEM((X_PLANES, 2, 16, 128), jnp.float32),
+            VMEM((Z_CORES, 16, 128), jnp.float32),
+            VMEM((Z_CORES, 16, 128), jnp.float32),
+            VMEM((16, 128), jnp.float32),
+            VMEM((2, STRIP + 1, 3, 8, 128), jnp.float32),
+            VMEM((2, STRIP, 3, 8, 128), jnp.float32),
+            VMEM((2, STRIP, 3, 8, 128), jnp.float32),
+            VMEM((STRIP, 3, 8, 128), jnp.float32),
+            VMEM((STRIP, 8, 128), jnp.float32),
+            VMEM((STEPS, 2, 2, 8, 8, 128), jnp.float32),
+            VMEM((STEPS, 2, 2, 3, 8, 128), jnp.float32),
+            VMEM((2, 3, 384, 128), jnp.float32),
+            VMEM((3, 384, 128), jnp.float32),
+            VMEM((2, 3, 384, 128), jnp.float32),
             VMEM((6, 2, 96, 128), jnp.float32),
             VMEM((6, 2, 96, 128), jnp.float32),
             VMEM((6, 2, 48, 128), jnp.float32),
             VMEM((2, 3, 384, 128), jnp.float32),
-            *sems,
-            pltpu.SemaphoreType.DMA((2, 3)),
+            dma((9,)),
+            dma((X_PLANES - 1,)),
+            dma((X_PLANES - 1,)),
+            dma((Z_CORES - 1,)),
+            dma((Z_CORES - 1,)),
+            dma((6, 2)),
+            dma((6, 2)),
+            *([dma((6,))] * 6),
+            dma((2, 3)),
         ],
         compiler_params=pltpu.CompilerParams(
-            collective_id=2, has_side_effects=True, vmem_limit_bytes=40 << 20
+            collective_id=1, has_side_effects=True, vmem_limit_bytes=40 << 20
         ),
-        name="reduce",
-    )(peak)
+        name="coast",
+    )(nest_host, pick, edges, source, depth)
 
 
 def body(outer_source, outer_depth, wet_tiles, nest_host, nest_anchor, nest_source, nest_depth):
@@ -682,9 +670,7 @@
     depth = outer_depth.reshape(16, 8, 1024)
     halos = exchange_halos(eta, depth)
     level, flux, edges, pick = outer_steps(wet_tiles, nest_host, nest_anchor, eta, depth, halos)
-    own = route_edges(nest_host, pick, edges)
-    peak = advance_nests(own, nest_source, nest_depth)
-    mean, var = reduce_members(peak)
+    mean, var = advance_coast(nest_host, pick, edges, nest_source, nest_depth)
     return (level.reshape(2, 128, 1024), flux.reshape(2, 2, 128, 1024), mean, var)
 
 

time: 91 us -> 80.3 us (0.88)
  Pallas kernels: 81.4 us -> 70.9 us
    pallas_call x3 -> x1, Pallas kernels: 56.4 us -> 45.9 us  [advance_coast(): pl.pallas_call(coast_kernel, out_shape=(shape, shape), in_specs=[smem_spe...]
    unnamed x28 -> x22, local copies, waits for them, and re-layouts: 8.42 us -> 8.19 us
where the time goes in v3:
time: 80.3 us; the launch traced here: 79.8 us
  Pallas kernels  70.9 us (88%)
  local copies, waits for them, and re-layouts  8.19 us (10%)
    pallas_call x1, Pallas kernels, advance_coast(): pl.pallas_call(coast_kernel, out_shape=(shape, shape), in_specs=[smem_spe...  45.9 us
    pallas_call x1, Pallas kernels, outer_steps(): pl.pallas_call(outer_kernel, out_shape=(jax.ShapeDtypeStruct((2, 16, 8, 1...  14.7 us
    pallas_call x1, Pallas kernels, exchange_halos(): pl.pallas_call(halo_kernel, out_shape=(rows, rows, coef, coef), in_specs=...  10.3 us
    unnamed x22, local copies, waits for them, and re-layouts  8.19 us

profile of v3, /device:TPU:1, one launch (start us, length us, event | category | flops | bytes accessed | tf_op | source)
XLA Modules:
  0.0 79.8 jit_solution(16653391008223406493)
XLA Ops:
  0.6 0.0 copy-start.3
  0.6 0.0 copy-start
  0.7 0.9 %copy.11.wet_ref = s32[64,8]{1,0:T(8,128)S(1)} copy(s32[64,8]{0,1:T(8,128)} %param.9) | data formatting | bytes 4096 | tf_op args[2]
  1.5 0.8 copy.12.anchor_ref
  2.3 10.3 %halo.1 = (f32[2,8,1024]{2,1,0:T(8,128)}, f32[2,8,1024]{2,1,0:T(8,128)}, f32[8,1024]{1,0:T(8,128)}, f32[8,1024]{1,0:T(8,128)}) custom-call(f32[2,16,8,1024]{3,2,1,0:T(8,128)} %bitcast.4, f32[16,8,1024]{2,1,0:T(8,128)} %bitcast.6), custom_call_target="tpu_custom_call" | custom-call | tf_op jit(solution)/shard_map/halo/pallas_call | solution.py:65
  12.7 0.0 copy-done
  12.7 0.0 copy-start.1
  12.7 1.0 %copy-done.1 = f32[128,1024]{1,0:T(8,128)S(1)} copy-done((f32[128,1024]{1,0:T(8,128)S(1)}, f32[128,1024]{1,0:T(8,128)}, u32[]{:S(2)}) %copy-start.1) | copy-done | bytes 524312
  13.7 0.0 copy-start.4
  13.7 0.8 %copy-done.4 = f32[2,8,1024]{2,1,0:T(8,128)S(1)} copy-done((f32[2,8,1024]{2,1,0:T(8,128)S(1)}, f32[2,8,1024]{2,1,0:T(8,128)}, u32[]{:S(2)}) %copy-start.4) | copy-done | bytes 65560
  14.5 0.0 copy-start.5
  14.5 0.8 %copy-done.5 = f32[2,8,1024]{2,1,0:T(8,128)S(1)} copy-done((f32[2,8,1024]{2,1,0:T(8,128)S(1)}, f32[2,8,1024]{2,1,0:T(8,128)}, u32[]{:S(2)}) %copy-start.5) | copy-done | bytes 65560
  15.4 0.0 copy-start.6
  15.4 0.8 copy-done.6
  16.1 0.0 copy-start.7
  16.1 0.8 copy-done.7
  16.9 0.0 copy-start.8
  16.9 0.7 copy-done.8
  17.6 0.0 copy-start.2
  17.6 14.7 %outer.1 = (f32[2,16,8,1024]{3,2,1,0:T(8,128)}, f32[2,2,16,8,1024]{4,3,2,1,0:T(8,128)}, f32[2,16,128]{2,1,0:T(8,128)S(1)}, s32[64]{0:T(128)S(1)}) custom-call(s32[64,8]{1,0:T(8,128)S(1)} %copy.11.wet_ref, s32[64]{0:T(128)S(1)} %copy-done.8, s32[64,2]{1,0:T(8,128)S(1)} %copy.12.anchor_ref, f32[2,16,8,1024]{3,2,1,0:T(8,128)S(1)} %bitcast.5, ...), custom_call_target="tpu_custom_call" | custom-call | tf_op jit(solution)/shard_map/outer/pallas_call | solution.py:235
  32.2 0.0 copy-done.3
  32.3 0.0 copy-done.2
  32.3 45.9 %coast.1 = (f32[1,384,384]{2,1,0:T(8,128)S(1)}, f32[1,384,384]{2,1,0:T(8,128)S(1)}) custom-call(s32[64]{0:T(128)S(1)} %copy-done.8, s32[64]{0:T(128)S(1)} %get-tuple-element.20.pick_ref, f32[2,16,128]{2,1,0:T(8,128)S(1)} %get-tuple-element.21.edges_ref, f32[2,1,384,384]{3,2,1,0:T(8,128)S(1)} %copy-done.2, f32[1,384,384]{2,1,0:T(8,128)S(1)} %copy-done.3), custom_call_target="tpu_custom_call" | custom-call | tf_op jit(solution)/shard_map/coast/pallas_call | solution.py:627
  78.2 0.8 %copy.15 = f32[1,384,384]{2,1,0:T(8,128)} copy(f32[1,384,384]{2,1,0:T(8,128)S(1)} %get-tuple-element.30) | data formatting | bytes 1179648
  79.0 0.8 %copy.16 = f32[1,384,384]{2,1,0:T(8,128)} copy(f32[1,384,384]{2,1,0:T(8,128)S(1)} %get-tuple-element.31) | data formatting | bytes 1179648
Async XLA Ops:
  0.6 31.6 %copy-start.3 = (f32[1,384,384]{2,1,0:T(8,128)S(1)}, f32[1,384,384]{2,1,0:T(8,128)}, u32[]{:S(2)}) copy-start(f32[1,384,384]{2,1,0:T(8,128)} %depth_ref.1) | copy-start | bytes 1769476
  0.6 12.0 %copy-start = (f32[2,128,1024]{2,1,0:T(8,128)S(1)}, f32[2,128,1024]{2,1,0:T(8,128)}, u32[]{:S(2)}) copy-start(f32[2,128,1024]{2,1,0:T(8,128)} %param.7) | copy-start | bytes 3145732
  12.7 1.0 %copy-start.1 = (f32[128,1024]{1,0:T(8,128)S(1)}, f32[128,1024]{1,0:T(8,128)}, u32[]{:S(2)}) copy-start(f32[128,1024]{1,0:T(8,128)} %param.8) | copy-start | bytes 1572868
  13.7 0.8 %copy-start.4 = (f32[2,8,1024]{2,1,0:T(8,128)S(1)}, f32[2,8,1024]{2,1,0:T(8,128)}, u32[]{:S(2)}) copy-start(f32[2,8,1024]{2,1,0:T(8,128)} %get-tuple-element.14.up_eta) | copy-start | bytes 196612
  14.5 0.8 %copy-start.5 = (f32[2,8,1024]{2,1,0:T(8,128)S(1)}, f32[2,8,1024]{2,1,0:T(8,128)}, u32[]{:S(2)}) copy-start(f32[2,8,1024]{2,1,0:T(8,128)} %get-tuple-element.15.dn_eta) | copy-start | bytes 196612
  15.4 0.8 copy-start.6
  16.1 0.8 copy-start.7
  16.9 0.7 copy-start.8
  17.6 14.7 %copy-start.2 = (f32[2,1,384,384]{3,2,1,0:T(8,128)S(1)}, f32[2,1,384,384]{3,2,1,0:T(8,128)}, u32[]{:S(2)}) copy-start(f32[2,1,384,384]{3,2,1,0:T(8,128)} %source_ref.1) | copy-start | bytes 3538948

commit v4 on v3

--- a/solution.py
+++ b/solution.py
@@ -14,7 +14,6 @@
 STRIP = 48
 BATCH = 48
 VMEM = pltpu.VMEM
-ANY = pl.ANY
 
 
 def vmem_spec():
@@ -25,8 +24,8 @@
     return pl.BlockSpec(memory_space=pltpu.SMEM)
 
 
-def any_spec():
-    return pl.BlockSpec(memory_space=pl.ANY)
+def hbm_spec():
+    return pl.BlockSpec(memory_space=pltpu.HBM)
 
 
 def halo_kernel(eta_ref, depth_ref, up_eta, dn_eta, up_depth, dn_depth, send_sem, recv_sem):
@@ -37,11 +36,13 @@
     for peer in (below, above):
         pl.semaphore_signal(barrier, inc=1, device_id={"sec": peer}, device_id_type=MESH)
     pl.semaphore_wait(barrier, 2)
+    bottom = pl.ds(960, 64)
+    top = pl.ds(0, 64)
     plan = (
-        (eta_ref.at[:, 15], up_eta, below),
-        (eta_ref.at[:, 0], dn_eta, above),
-        (depth_ref.at[15], up_depth, below),
-        (depth_ref.at[0], dn_depth, above),
+        (eta_ref.at[:, bottom, :], up_eta, below),
+        (eta_ref.at[:, top, :], dn_eta, above),
+        (depth_ref.at[bottom, :], up_depth, below),
+        (depth_ref.at[top, :], dn_depth, above),
     )
     copies = []
     for number, (source, target, peer) in enumerate(plan):
@@ -60,200 +61,270 @@
 
 
 def exchange_halos(eta, depth):
-    rows = jax.ShapeDtypeStruct((2, 8, 1024), jnp.float32)
-    coef = jax.ShapeDtypeStruct((8, 1024), jnp.float32)
+    rows = jax.ShapeDtypeStruct((2, 64, 128), jnp.float32)
+    coef = jax.ShapeDtypeStruct((64, 128), jnp.float32)
     return pl.pallas_call(
         halo_kernel,
         out_shape=(rows, rows, coef, coef),
-        in_specs=[any_spec()] * 2,
-        out_specs=(any_spec(),) * 4,
+        in_specs=[hbm_spec()] * 2,
+        out_specs=(hbm_spec(),) * 4,
         scratch_shapes=[pltpu.SemaphoreType.DMA((4,)), pltpu.SemaphoreType.DMA((4,))],
         compiler_params=pltpu.CompilerParams(collective_id=0, has_side_effects=True),
         name="halo",
     )(eta, depth)
 
 
+LOW = 2
+ROWS_HELD = 21
+
+
 def outer_kernel(
-    wet_ref, host_ref, anchor_ref, eta_in, depth_in, up_eta, dn_eta, up_depth, dn_depth,
-    level_ref, flux_ref, edges_ref, pick_ref,
-    eta, fx, fy, dw, masks, first, last,
+    wet_hbm, host_hbm, anchor_hbm, eta_hbm, depth_hbm, up_eta_hbm, dn_eta_hbm, up_depth_hbm, dn_depth_hbm,
+    level_hbm, flux_hbm, edges_ref, pick_ref,
+    eta_in, depth_in, up_eta, dn_eta, up_depth, dn_depth, wet, host, anchor,
+    eta, fx, fy, dw, masks, levels, flux_out, first, last,
+    in_sem, out_sem,
 ):
     section = lax.axis_index("sec")
-    lanes = lax.broadcasted_iota(jnp.int32, (8, 1024), 1)
-    subs = lax.broadcasted_iota(jnp.int32, (8, 1024), 0)
+    lane = lane_ids()
+    sub = sub_ids()
+    loads = [
+        pltpu.make_async_copy(source, target, in_sem.at[number])
+        for number, (source, target) in enumerate(
+            (
+                (wet_hbm, wet),
+                (host_hbm, host),
+                (anchor_hbm, anchor),
+                (depth_hbm, depth_in),
+                (up_depth_hbm, up_depth),
+                (dn_depth_hbm, dn_depth),
+                (eta_hbm, eta_in),
+                (up_eta_hbm, up_eta),
+                (dn_eta_hbm, dn_eta),
+            )
+        )
+    ]
+    for copy in loads:
+        copy.start()
+    for copy in loads[:3]:
+        copy.wait()
 
     first[section] = 0
     last[section] = 0
 
     def note(n, _):
-        last[host_ref[n]] = n
-        first[host_ref[SECTIONS - 1 - n]] = SECTIONS - 1 - n
+        last[host[n]] = n
+        first[host[SECTIONS - 1 - n]] = SECTIONS - 1 - n
         return 0
 
-    lax.fori_loop(0, SECTIONS, note, 0)
+    lax.fori_loop(0, SECTIONS, note, 0, unroll=8)
 
     def choose(n, _):
-        host = host_ref[n]
-        pick_ref[n] = (host // Z_CORES) * 2 + jnp.where(first[host] == n, 0, 1)
+        section_of = host[n]
+        pick_ref[n] = (section_of // Z_CORES) * 2 + jnp.where(first[section_of] == n, 0, 1)
         return 0
 
-    lax.fori_loop(0, SECTIONS, choose, 0)
-
-    for band in range(3):
-        row = section + band - 1
+    lax.fori_loop(0, SECTIONS, choose, 0, unroll=8)
+
+    def flag(row, t):
         inside = (row >= 0) & (row < SECTIONS)
-        row = jnp.clip(row, 0, SECTIONS - 1)
-        for tile in range(8):
-            flag = jnp.where(inside, wet_ref[row, tile], 0)
-            masks[band, :, tile * 128 : (tile + 1) * 128] = jnp.full(
-                (8, 128), flag, jnp.int32
-            ).astype(jnp.float32)
-    zeros = jnp.zeros((8, 1024), jnp.float32)
-    masks[3] = zeros
-
-    def band_of(k):
-        return jnp.where(k == 1, 0, jnp.where(k <= 17, 1, jnp.where(k == 18, 2, 3)))
-
-    for k, (rows, coef) in ((1, (up_eta, up_depth)), (18, (dn_eta, dn_depth))):
-        mask = masks[0 if k == 1 else 2]
-        dw[k] = mask * coef[...]
-        for m in range(2):
-            eta[m, k] = mask * rows[m]
-    dw[0] = zeros
-    for m in range(2):
-        for k in (0, 19):
-            eta[m, k] = zeros
-            fx[m, k] = zeros
-        fy[m, 0] = zeros
-        fy[m, 19] = zeros
-    dw[19] = zeros
-
-    def fill(k, _):
-        mask = masks[1]
-        dw[k + 2] = mask * depth_in[k]
-        for m in range(2):
-            eta[m, k + 2] = mask * eta_in[m, k]
-        return 0
-
-    lax.fori_loop(0, 16, fill, 0)
-
-    def east(x):
-        return jnp.where(lanes == 1023, 0.0, pltpu.roll(x, 1023, 1))
-
-    def west(x):
-        return jnp.where(lanes == 0, 0.0, pltpu.roll(x, 1, 1))
-
-    def south(x, following):
-        return jnp.where(subs == 7, pltpu.roll(following, 7, 0), pltpu.roll(x, 7, 0))
-
-    def north(x, previous):
-        return jnp.where(subs == 0, pltpu.roll(previous, 1, 0), pltpu.roll(x, 1, 0))
-
-    def sweep_first(k, _):
-        for m in range(2):
-            now = eta[m, k]
-            before = eta[m, k - 1]
-            fx[m, k] = -(dw[k] * (east(now) - now))
-            fy[m, k - 1] = -(dw[k - 1] * (south(before, now) - before))
-        return 0
-
-    def edges(step):
-        rows128 = (
-            lax.broadcasted_iota(jnp.int32, (16, 8, 128), 0) * 8
-            + lax.broadcasted_iota(jnp.int32, (16, 8, 128), 1)
-        )
-        lane16 = lax.broadcasted_iota(jnp.int32, (16, 8, 128), 2)
-        lane_row = lax.broadcasted_iota(jnp.int32, (8, 128), 1)
+        value = jnp.where(inside, wet[t, jnp.clip(row, 0, SECTIONS - 1)], 0)
+        return jnp.full((8, 128), value, jnp.int32).astype(jnp.float32)
+
+    for t in range(8):
+        own = flag(section, t)
+        masks[0, t] = jnp.where(sub == 0, flag(section - 1, t), own)
+        masks[1, t] = own
+        masks[2, t] = jnp.where(sub == 7, flag(section + 1, t), own)
+
+    def strip(ref, i, t):
+        return ref[pl.ds((i // 8) * 64 + t * 8 + i % 8, 8, stride=128), :]
+
+    def held(ref, before, after, i, t):
+        if i < 0:
+            edge = before[t * 8 + 8 + i : t * 8 + 9 + i, :]
+            return jnp.where(sub == 0, jnp.broadcast_to(edge, (8, 128)), pltpu.roll(strip(ref, i + 16, t), 1, 0))
+        if i > 15:
+            edge = after[t * 8 + i - 16 : t * 8 + i - 15, :]
+            return jnp.where(sub == 7, jnp.broadcast_to(edge, (8, 128)), pltpu.roll(strip(ref, i - 16, t), 7, 0))
+        return strip(ref, i, t)
+
+    def mask_of(i, t):
+        return masks[0 if i < 0 else 1 if i < 16 else 2, t]
+
+    for copy in loads[3:6]:
+        copy.wait()
+    for i in range(-2, 18):
+        for t in range(8):
+            dw[i + LOW, t] = mask_of(i, t) * held(depth_in, up_depth, dn_depth, i, t)
+
+    def east_change(now):
+        rolled = [pltpu.roll(now[t], 127, 1) for t in range(8)]
+        out = []
+        for t in range(8):
+            beyond = jnp.where(lane == 127, 0.0 if t == 7 else rolled[t + 1], rolled[t])
+            out.append(beyond - now[t])
+        return out
+
+    def west_change(flow):
+        rolled = [pltpu.roll(flow[t], 1, 1) for t in range(8)]
+        out = []
+        for t in range(8):
+            behind = jnp.where(lane == 0, 0.0 if t == 0 else rolled[t - 1], rolled[t])
+            out.append(flow[t] - behind)
+        return out
+
+    def place(ref, i, t, value):
+        ref[pl.ds((i // 8) * 64 + t * 8 + i % 8, 8, stride=128), :] = value
+
+    def edges(m, step):
+        level = levels.at[m]
         for slot in range(2):
             nest = (first if slot == 0 else last)[section]
-            r0 = anchor_ref[nest, 0]
-            c0 = anchor_ref[nest, 1]
-            base = pl.multiple_of(jnp.minimum(c0 // 128, 6) * 128, 128)
-            left = pl.multiple_of((c0 // 128) * 128, 128)
-            right = pl.multiple_of(((c0 + 63) // 128) * 128, 128)
-            for m in range(2):
-
-                def row_of(r):
-                    tile = r // 8 + 2
-                    x = eta[m, tile, pl.ds(lax.rem(r, 8), 1), pl.ds(base, 256)]
-                    return jnp.broadcast_to(x, (8, 256))
-
-                shift = c0 - base
-                top = pltpu.roll(row_of(r0), 256 - shift, 1)[:, :128]
-                bottom = pltpu.roll(row_of(r0 + 63), lax.rem(320 - shift, 256), 1)[:, :128]
-                pair = jnp.where(lane_row < 64, top, bottom)
-                at = (step * 2 + m) * 2
-                edges_ref[slot, at : at + 1, :] = pair[0:1]
-                west_block = eta[m, 2:18, :, pl.ds(left, 128)]
-                east_block = eta[m, 2:18, :, pl.ds(right, 128)]
-                west_col = jnp.sum(jnp.where(lane16 == c0 - left, west_block, 0.0), axis=2, keepdims=True)
-                east_col = jnp.sum(jnp.where(lane16 == c0 + 63 - right, east_block, 0.0), axis=2, keepdims=True)
-                place = rows128 - r0
-                both = jnp.where((lane16 == place) & (lane16 < 64), west_col, 0.0) + jnp.where(
-                    (lane16 == place + 64) & (lane16 >= 64), east_col, 0.0
+            r0 = anchor[0, nest]
+            c0 = anchor[1, nest]
+            shift = lax.rem(c0, 128)
+            t0 = c0 // 128
+            t1 = jnp.minimum(t0 + 1, 7)
+            t2 = (c0 + 63) // 128
+
+            def row_of(r, offset):
+                spot = lane - offset + shift
+                index = lax.rem(spot + 128, 128)
+                at = (r // 8) * 64 + lax.rem(r, 8)
+                here = jnp.broadcast_to(level[pl.ds(at + t0 * 8, 1), :], (8, 128))
+                there = jnp.broadcast_to(level[pl.ds(at + t1 * 8, 1), :], (8, 128))
+                return jnp.where(
+                    spot < 128,
+                    jnp.take_along_axis(here, index, axis=1),
+                    jnp.take_along_axis(there, index, axis=1),
                 )
-                edges_ref[slot, at + 1 : at + 2, :] = jnp.sum(jnp.sum(both, axis=0), axis=0, keepdims=True)
+
+            pair = jnp.where(lane < 64, row_of(r0, 0), row_of(r0 + 63, 64))
+            edges_ref[slot, m, 2 * step : 2 * step + 1, :] = pair[0:1]
+            total = jnp.zeros((8, 128), jnp.float32)
+            for tile in range(16):
+                west_block = level[pl.ds(pl.multiple_of(tile * 64 + t0 * 8, 8), 8), :]
+                east_block = level[pl.ds(pl.multiple_of(tile * 64 + t2 * 8, 8), 8), :]
+                west_col = jnp.take_along_axis(west_block, jnp.full((8, 128), shift, jnp.int32), axis=1)
+                east_col = jnp.take_along_axis(
+                    east_block, jnp.full((8, 128), lax.rem(c0 + 63, 128), jnp.int32), axis=1
+                )
+                column = jnp.where(lane < 64, west_col, east_col)
+                row = tile * 8 + sub - r0
+                wanted = (row >= 0) & (row < 64) & (lax.rem(lane, 64) == row)
+                total = total + jnp.where(wanted, column, 0.0)
+            edges_ref[slot, m, 2 * step + 1 : 2 * step + 2, :] = jnp.sum(total, axis=0, keepdims=True)
 
     for slot in range(2):
-        edges_ref[slot, 12:16, :] = jnp.zeros((4, 128), jnp.float32)
-    lax.fori_loop(1, 20, sweep_first, 0)
-    edges(0)
-
-    def full_step(step):
-        def body(k, carry):
-            new_carry = []
-            mask = masks[band_of(k)]
-            for m in range(2):
-                px = fx[m, k]
-                py = fy[m, k]
-                py_before = carry[m]
-                before = eta[m, k - 1]
-                now = mask * (eta[m, k] - (px - west(px)) - (py - north(py, py_before)))
-                eta[m, k] = now
-                fx[m, k] = px - dw[k] * (east(now) - now)
-                fy[m, k - 1] = py_before - dw[k - 1] * (south(before, now) - before)
-                new_carry.append(py)
-            return tuple(new_carry)
-
-        lax.fori_loop(1, 20, body, (zeros, zeros))
-        edges(step)
-
-    full_step(1)
-    full_step(2)
-
-    def emit(k, _):
         for m in range(2):
-            level_ref[m, k] = eta[m, k + 2]
-            flux_ref[0, m, k] = fx[m, k + 2]
-            flux_ref[1, m, k] = fy[m, k + 2]
+            edges_ref[slot, m, 6:8, :] = jnp.zeros((2, 128), jnp.float32)
+    for copy in loads[6:]:
+        copy.wait()
+
+    def member(m, _):
+        before = None
+        for i in range(-2, 19):
+            now = [
+                mask_of(i, t) * held(eta_in.at[m], up_eta.at[m], dn_eta.at[m], i, t) for t in range(8)
+            ]
+            change = east_change(now) if -1 <= i <= 17 else None
+            for t in range(8):
+                eta[i + LOW, t] = now[t]
+                if 0 <= i <= 15:
+                    place(levels.at[m], i, t, now[t])
+                if change is not None:
+                    fx[i + LOW, t] = -(dw[i + LOW, t] * change[t])
+                if before is not None:
+                    fy[i - 1 + LOW, t] = -(dw[i - 1 + LOW, t] * (now[t] - before[t]))
+            before = now
+        edges(m, 0)
+
+        for step, low, high in ((1, -1, 17), (2, 0, 16)):
+            before = None
+            flow_before = [fy[low - 1 + LOW, t] for t in range(8)]
+            for i in range(low, high + 1):
+                px = [fx[i + LOW, t] for t in range(8)]
+                py = [fy[i + LOW, t] for t in range(8)]
+                leave = west_change(px)
+                now = [
+                    mask_of(i, t) * (eta[i + LOW, t] - leave[t] - (py[t] - flow_before[t])) for t in range(8)
+                ]
+                change = east_change(now) if (0 if step == 1 else low) <= i < high or step == 1 else None
+                for t in range(8):
+                    if step == 1:
+                        eta[i + LOW, t] = now[t]
+                    if 0 <= i <= 15:
+                        place(levels.at[m], i, t, now[t])
+                    if change is not None:
+                        value = px[t] - dw[i + LOW, t] * change[t]
+                        if step == 1:
+                            fx[i + LOW, t] = value
+                        else:
+                            place(flux_out.at[0, m], i, t, value)
+                    if before is not None:
+                        value = flow_before[t] - dw[i - 1 + LOW, t] * (now[t] - before[t])
+                        if step == 1:
+                            fy[i - 1 + LOW, t] = value
+                        else:
+                            place(flux_out.at[1, m], i - 1, t, value)
+                before = now
+                flow_before = py
+            if step == 2:
+                pltpu.make_async_copy(levels.at[m], level_hbm.at[m], out_sem.at[0, m]).start()
+                for side in range(2):
+                    pltpu.make_async_copy(
+                        flux_out.at[side, m], flux_hbm.at[side, m], out_sem.at[1 + side, m]
+                    ).start()
+            edges(m, step)
         return 0
 
-    lax.fori_loop(0, 16, emit, 0)
+    lax.fori_loop(0, 2, member, 0)
+    for m in range(2):
+        pltpu.make_async_copy(levels.at[m], level_hbm.at[m], out_sem.at[0, m]).wait()
+        for side in range(2):
+            pltpu.make_async_copy(
+                flux_out.at[side, m], flux_hbm.at[side, m], out_sem.at[1 + side, m]
+            ).wait()
 
 
 def outer_steps(wet_tiles, nest_host, nest_anchor, eta, depth, halos):
+    f32 = jnp.float32
     return pl.pallas_call(
         outer_kernel,
         out_shape=(
-            jax.ShapeDtypeStruct((2, 16, 8, 1024), jnp.float32),
-            jax.ShapeDtypeStruct((2, 2, 16, 8, 1024), jnp.float32),
-            jax.ShapeDtypeStruct((2, 16, 128), jnp.float32),
+            jax.ShapeDtypeStruct((2, 1024, 128), f32),
+            jax.ShapeDtypeStruct((2, 2, 1024, 128), f32),
+            jax.ShapeDtypeStruct((2, 2, 8, 128), f32),
             jax.ShapeDtypeStruct((SECTIONS,), jnp.int32),
         ),
-        in_specs=[smem_spec()] * 3 + [vmem_spec()] * 6,
-        out_specs=(vmem_spec(), vmem_spec(), vmem_spec(), smem_spec()),
+        in_specs=[hbm_spec()] * 9,
+        out_specs=(hbm_spec(), hbm_spec(), vmem_spec(), smem_spec()),
         scratch_shapes=[
-            VMEM((2, 20, 8, 1024), jnp.float32),
-            VMEM((2, 20, 8, 1024), jnp.float32),
-            VMEM((2, 20, 8, 1024), jnp.float32),
-            VMEM((20, 8, 1024), jnp.float32),
-            VMEM((4, 8, 1024), jnp.float32),
+            VMEM((2, 1024, 128), f32),
+            VMEM((1024, 128), f32),
+            VMEM((2, 64, 128), f32),
+            VMEM((2, 64, 128), f32),
+            VMEM((64, 128), f32),
+            VMEM((64, 128), f32),
+            pltpu.SMEM((8, SECTIONS), jnp.int32),
+            pltpu.SMEM((SECTIONS,), jnp.int32),
+            pltpu.SMEM((2, SECTIONS), jnp.int32),
+            VMEM((ROWS_HELD, 8, 8, 128), f32),
+            VMEM((ROWS_HELD, 8, 8, 128), f32),
+            VMEM((ROWS_HELD, 8, 8, 128), f32),
+            VMEM((ROWS_HELD, 8, 8, 128), f32),
+            VMEM((3, 8, 8, 128), f32),
+            VMEM((2, 1024, 128), f32),
+            VMEM((2, 2, 1024, 128), f32),
             pltpu.SMEM((SECTIONS,), jnp.int32),
             pltpu.SMEM((SECTIONS,), jnp.int32),
+            pltpu.SemaphoreType.DMA((9,)),
+            pltpu.SemaphoreType.DMA((3, 2)),
         ],
-        compiler_params=pltpu.CompilerParams(vmem_limit_bytes=40 << 20),
+        compiler_params=pltpu.CompilerParams(vmem_limit_bytes=62 << 20),
         name="outer",
-    )(wet_tiles, nest_host, nest_anchor, eta, depth, *halos)
+    )(wet_tiles.T, nest_host, nest_anchor.T, eta, depth, *halos)
 
 
 def lane_ids():
@@ -298,7 +369,7 @@
 
     for step in steps:
         for m in range(2):
-            at = (step * 2 + m) * 2
+            at = m * 8 + step * 2
             level = edge_ref[at : at + 1, :]
             upright = edge_ref[at + 1 : at + 2, :]
             for q in range(8):
@@ -627,8 +698,8 @@
     return pl.pallas_call(
         coast_kernel,
         out_shape=(shape, shape),
-        in_specs=[smem_spec(), smem_spec(), vmem_spec(), any_spec(), any_spec()],
-        out_specs=(any_spec(), any_spec()),
+        in_specs=[smem_spec(), smem_spec(), vmem_spec(), hbm_spec(), hbm_spec()],
+        out_specs=(hbm_spec(), hbm_spec()),
         scratch_shapes=[
             VMEM((X_PLANES, 2, 16, 128), jnp.float32),
             VMEM((Z_CORES, 16, 128), jnp.float32),
@@ -659,19 +730,34 @@
             dma((2, 3)),
         ],
         compiler_params=pltpu.CompilerParams(
-            collective_id=1, has_side_effects=True, vmem_limit_bytes=40 << 20
+            collective_id=1, has_side_effects=True, vmem_limit_bytes=62 << 20
         ),
         name="coast",
     )(nest_host, pick, edges, source, depth)
 
 
+def tiled(field):
+    lead = field.shape[:-2]
+    n = len(lead)
+    split = field.reshape(*lead, 16, 8, 8, 128)
+    return jnp.swapaxes(split, n + 1, n + 2).reshape(*lead, 1024, 128)
+
+
+def untiled(field):
+    lead = field.shape[:-2]
+    n = len(lead)
+    split = field.reshape(*lead, 16, 8, 8, 128)
+    return jnp.swapaxes(split, n + 1, n + 2).reshape(*lead, 128, 1024)
+
+
 def body(outer_source, outer_depth, wet_tiles, nest_host, nest_anchor, nest_source, nest_depth):
-    eta = outer_source.reshape(2, 16, 8, 1024)
-    depth = outer_depth.reshape(16, 8, 1024)
+    eta = tiled(outer_source)
+    depth = tiled(outer_depth)
     halos = exchange_halos(eta, depth)
     level, flux, edges, pick = outer_steps(wet_tiles, nest_host, nest_anchor, eta, depth, halos)
+    edges = edges.reshape(2, 16, 128)
     mean, var = advance_coast(nest_host, pick, edges, nest_source, nest_depth)
-    return (level.reshape(2, 128, 1024), flux.reshape(2, 2, 128, 1024), mean, var)
+    return (untiled(level), untiled(flux), mean, var)
 
 
 def solution(mesh):

time: 80.3 us -> 74.7 us (0.930)
  local copies, waits for them, and re-layouts: 8.19 us -> 3.83 us
  Pallas kernels: 70.9 us -> 69.8 us
    unnamed x22 -> x2, local copies, waits for them, and re-layouts: 8.19 us -> 3.83 us
    pallas_call x1, Pallas kernels: 14.7 us -> 12.8 us  [outer_steps(): pl.pallas_call(outer_kernel, out_shape=(jax.ShapeDtypeStruct((2, 1024, 12...]
where the time goes in v4:
time: 74.7 us; the launch traced here: 74.3 us
  Pallas kernels  69.8 us (93%)
  local copies, waits for them, and re-layouts  3.83 us (5%)
    pallas_call x1, Pallas kernels, advance_coast(): pl.pallas_call(coast_kernel, out_shape=(shape, shape), in_specs=[smem_spe...  46.7 us
    pallas_call x1, Pallas kernels, outer_steps(): pl.pallas_call(outer_kernel, out_shape=(jax.ShapeDtypeStruct((2, 1024, 12...  12.8 us
    pallas_call x1, Pallas kernels, exchange_halos(): pl.pallas_call(halo_kernel, out_shape=(rows, rows, coef, coef), in_specs=...  10.4 us
    unnamed x2, local copies, waits for them, and re-layouts  3.83 us

profile of v4, /device:TPU:1, one launch (start us, length us, event | category | flops | bytes accessed | tf_op | source)
XLA Modules:
  0.0 74.3 jit_solution(16252403537527415274)
XLA Ops:
  0.6 10.4 %halo.1 = (f32[2,64,128]{2,1,0:T(8,128)}, f32[2,64,128]{2,1,0:T(8,128)}, f32[64,128]{1,0:T(8,128)}, f32[64,128]{1,0:T(8,128)}) custom-call(f32[2,1024,128]{2,1,0:T(8,128)} %bitcast.23, f32[1024,128]{1,0:T(8,128)} %bitcast.25), custom_call_target="tpu_custom_call" | custom-call | tf_op jit(solution)/shard_map/halo/pallas_call | solution.py:66
  11.0 12.8 %outer.1 = (f32[2,1024,128]{2,1,0:T(8,128)}, f32[2,2,1024,128]{3,2,1,0:T(8,128)}, f32[2,2,8,128]{3,2,1,0:T(8,128)}, s32[64]{0:T(128)}) custom-call(s32[8,64]{1,0:T(8,128)} %bitcast.28, s32[64]{0:T(128)} %host_ref.1, s32[2,64]{1,0:T(2,128)} %bitcast.29, f32[2,1024,128]{2,1,0:T(8,128)} %bitcast.24, f32[1024,128]{1,0:T(8,128)} %bitcast.26, ...), custom_call_target="tpu_custom_call" | custom-call | tf_op jit(solution)/shard_map/outer/pallas_call | solution.py:293
  23.8 46.7 %coast.1 = (f32[1,384,384]{2,1,0:T(8,128)}, f32[1,384,384]{2,1,0:T(8,128)}) custom-call(s32[64]{0:T(128)} %host_ref.1, s32[64]{0:T(128)} %get-tuple-element.20.pick_ref, f32[2,16,128]{2,1,0:T(8,128)} %bitcast.27, f32[2,1,384,384]{3,2,1,0:T(8,128)} %source_ref.1, f32[1,384,384]{2,1,0:T(8,128)} %depth_ref.1), custom_call_target="tpu_custom_call" | custom-call | tf_op jit(solution)/shard_map/coast/pallas_call | solution.py:698
  70.5 1.9 %copy.13 = f32[1,384,384]{2,1,0:T(8,128)} copy(f32[1,384,384]{2,1,0:T(8,128)} %get-tuple-element.30) | data formatting | bytes 1179648
  72.4 1.9 %copy.14 = f32[1,384,384]{2,1,0:T(8,128)} copy(f32[1,384,384]{2,1,0:T(8,128)} %get-tuple-element.31) | data formatting | bytes 1179648

commit v5 on v4

--- a/solution.py
+++ b/solution.py
@@ -201,7 +201,9 @@
                 )
 
             pair = jnp.where(lane < 64, row_of(r0, 0), row_of(r0 + 63, 64))
-            edges_ref[slot, m, 2 * step : 2 * step + 1, :] = pair[0:1]
+            part = 0 if step == 0 else 1
+            at = 2 * m + (4 if step == 2 else 0)
+            edges_ref[slot, part, pl.ds(at, 1), :] = pair[0:1]
             total = jnp.zeros((8, 128), jnp.float32)
             for tile in range(16):
                 west_block = level[pl.ds(pl.multiple_of(tile * 64 + t0 * 8, 8), 8), :]
@@ -214,11 +216,10 @@
                 row = tile * 8 + sub - r0
                 wanted = (row >= 0) & (row < 64) & (lax.rem(lane, 64) == row)
                 total = total + jnp.where(wanted, column, 0.0)
-            edges_ref[slot, m, 2 * step + 1 : 2 * step + 2, :] = jnp.sum(total, axis=0, keepdims=True)
+            edges_ref[slot, part, pl.ds(at + 1, 1), :] = jnp.sum(total, axis=0, keepdims=True)
 
     for slot in range(2):
-        for m in range(2):
-            edges_ref[slot, m, 6:8, :] = jnp.zeros((2, 128), jnp.float32)
+        edges_ref[slot, 0, 4:8, :] = jnp.zeros((4, 128), jnp.float32)
     for copy in loads[6:]:
         copy.wait()
 
@@ -369,7 +370,7 @@
 
     for step in steps:
         for m in range(2):
-            at = m * 8 + step * 2
+            at = m * 2 + (4 if step == 2 else 0)
             level = edge_ref[at : at + 1, :]
             upright = edge_ref[at + 1 : at + 2, :]
             for q in range(8):
@@ -483,7 +484,7 @@
     lax.fori_loop(low, high, substep, 0)
 
 
-def store_peak(peak, peak_ref, rows, m):
+def settle_peak(peak, rows, m):
     sub = sub_ids()
     for t in range(3):
         for side, i, edge_sub in ((0, 0, 0), (1, STRIP - 1, 7)):
@@ -492,21 +493,13 @@
             )
             peak[m, i, t] = jnp.where(sub == edge_sub, top, peak[m, i, t])
 
-    def store(i, _):
-        parts = straighten([peak[m, i, t] for t in range(3)])
-        for t in range(3):
-            peak_ref[m, t, pl.ds(i, 8, stride=STRIP), :] = parts[t]
-        return 0
-
-    lax.fori_loop(0, STRIP, store, 0, unroll=4)
-
 
 def coast_kernel(
     host_ref, pick_ref, edges_ref, source_ref, depth_ref, mean_ref, var_ref,
-    gathered, outgoing, incoming, own_edge,
-    h, div, peak, coef, d2, cols, rows, src, dsrc, pn,
+    gathered, outgoing, incoming_first, incoming_later, own_edge,
+    h, div, peak, coef, d2, cols, rows, src, dsrc,
     r1, st, r2, mv,
-    load_sem, send_x, recv_x, send_z, recv_z, s1, q1, s2, q2, s3, q3, s4, q4, osem,
+    load_sem, send_x, recv_x, send_z, recv_z, s1, q1, s2, q2, s3, q3, s4, q4,
 ):
     sec = lax.axis_index("sec")
     plane = sec // Z_CORES
@@ -563,41 +556,55 @@
     for copy in along_x:
         copy.wait()
     along_z = []
-    for step in range(Z_CORES):
-        target = lax.rem(spot + step, Z_CORES)
-        choice = pick_ref[plane * Z_CORES + target]
-        message = gathered[choice // 2, lax.rem(choice, 2)]
-        if step == 0:
-            incoming[spot] = message
-            continue
-        outgoing[step] = message
-        copy = pltpu.make_async_remote_copy(
-            src_ref=outgoing.at[step],
-            dst_ref=incoming.at[spot],
-            send_sem=send_z.at[step - 1],
-            recv_sem=recv_z.at[step - 1],
-            device_id={"sec": plane * Z_CORES + target},
-            device_id_type=MESH,
-        )
-        copy.start()
-        along_z.append(copy)
+    incoming = (incoming_first, incoming_later)
+    for part in range(2):
+        for step in range(Z_CORES):
+            target = lax.rem(spot + step, Z_CORES)
+            choice = pick_ref[plane * Z_CORES + target]
+            message = gathered[choice // 2, lax.rem(choice, 2), part]
+            if step == 0:
+                incoming[part][spot] = message
+                continue
+            outgoing[part, step] = message
+            copy = pltpu.make_async_remote_copy(
+                src_ref=outgoing.at[part, step],
+                dst_ref=incoming[part].at[spot],
+                send_sem=send_z.at[part, step - 1],
+                recv_sem=recv_z.at[part, step - 1],
+                device_id={"sec": plane * Z_CORES + target},
+                device_id_type=MESH,
+            )
+            copy.start()
+            along_z.append(copy)
     for copy in loads[3:]:
         copy.wait()
     for m in range(2):
         load_source(src, h, div, m)
-    for copy in along_z:
-        copy.wait()
-    own_edge[...] = incoming[lax.rem(host_ref[sec], Z_CORES)]
-    spread_edges(own_edge, cols, rows, range(STEPS))
+    host_spot = lax.rem(host_ref[sec], Z_CORES)
+    for copy in along_z[: Z_CORES - 1]:
+        copy.wait_recv()
+    own_edge[0] = incoming_first[host_spot]
+    spread_edges(own_edge.at[0], cols, rows, (0,))
+
+    def early(m, _):
+        first_substep(h, peak, cols, rows, m)
+        substeps(m, 1, REFINE, h, div, peak, coef, d2, cols, rows)
+        return 0
+
+    lax.fori_loop(0, 2, early, 0)
+    for copy in along_z[Z_CORES - 1 :]:
+        copy.wait_recv()
+    own_edge[1] = incoming_later[host_spot]
+    spread_edges(own_edge.at[1], cols, rows, (1, 2))
 
     one = (near, far)
     two = (far, near)
     keep1 = (gray, high)
     keep2 = (high, gray)
-    flows = [(t, half) for t in range(3) for half in range(2)]
-
-    def rows_of(half, bit1):
-        return pl.multiple_of(half * 192 + bit1 * 96, 8)
+    flows = [(chunk, half) for chunk in range(3) for half in range(2)]
+
+    def quad(chunk, half, bit1):
+        return half * 24 + chunk * 8 + bit1 * 4
 
     def remote(src_ref, dst_ref, send, recv, peer):
         return pltpu.make_async_remote_copy(
@@ -605,106 +612,115 @@
             device_id={"mem": peer}, device_id_type=MESH,
         )
 
-    first = {}
-    for m in range(2):
-        first_substep(h, peak, cols, rows, m)
-        substeps(m, 1, STEPS * REFINE, h, div, peak, coef, d2, cols, rows)
-        store_peak(peak, pn, rows, m)
-        for t, half in flows:
-            n = 2 * t + half
-            away = pl.ds(rows_of(half, 1 - keep1[half]), 96)
-            first[m, n] = remote(pn.at[m, t, away, :], r1.at[n, m], s1.at[n, m], q1.at[n, m], one[half])
-            first[m, n].start()
+    def first(m, chunk, half):
+        n = 2 * chunk + half
+        away = pl.ds(quad(chunk, half, 1 - keep1[half]), 4)
+        return remote(peak.at[m, away], r1.at[n, m], s1.at[n, m], q1.at[n, m], one[half])
+
+    def late(m, _):
+        substeps(m, REFINE, STEPS * REFINE, h, div, peak, coef, d2, cols, rows)
+        settle_peak(peak, rows, m)
+        for chunk, half in flows:
+            first(m, chunk, half).start()
+        return 0
+
+    lax.fori_loop(0, 2, late, 0)
 
     second = {}
-    for t, half in flows:
-        n = 2 * t + half
+    for chunk, half in flows:
+        n = 2 * chunk + half
         for m in range(2):
-            first[m, n].wait_recv()
-        kept = rows_of(half, keep1[half])
-
-        def merge_part(part, n=n, t=t, kept=kept):
-            for index in range(6):
-                local = pl.multiple_of(part * 48 + index * 8, 8)
-                here = pl.ds(pl.multiple_of(kept + local, 8), 8)
-                a = pn[0, t, here, :]
-                b = pn[1, t, here, :]
-                c = r1[n, 0, pl.ds(local, 8), :]
-                d = r1[n, 1, pl.ds(local, 8), :]
-                total = (a + b) + (c + d)
-                middle = total * 0.25
-                a = a - middle
-                b = b - middle
-                c = c - middle
-                d = d - middle
-                st[n, 0, pl.ds(local, 8), :] = total
-                st[n, 1, pl.ds(local, 8), :] = (a * a + b * b) + (c * c + d * d)
-
-        merge_part(1 - keep2[half])
-        away = pl.ds(pl.multiple_of((1 - keep2[half]) * 48, 8), 48)
-        second[n] = remote(st.at[n, :, away, :], r2.at[n], s2.at[n], q2.at[n], two[half])
+            first(m, chunk, half).wait_recv()
+        kept = quad(chunk, half, keep1[half])
+
+        def merge_pair(bit2, n=n, kept=kept):
+            for r in range(2):
+                local = bit2 * 2 + r
+                for t in range(3):
+                    a = peak[0, kept + local, t]
+                    b = peak[1, kept + local, t]
+                    c = r1[n, 0, local, t]
+                    d = r1[n, 1, local, t]
+                    total = (a + b) + (c + d)
+                    middle = total * 0.25
+                    a = a - middle
+                    b = b - middle
+                    c = c - middle
+                    d = d - middle
+                    st[n, 0, local, t] = total
+                    st[n, 1, local, t] = (a * a + b * b) + (c * c + d * d)
+
+        merge_pair(1 - keep2[half])
+        away = pl.ds((1 - keep2[half]) * 2, 2)
+        second[n] = remote(st.at[n, :, away], r2.at[n], s2.at[n], q2.at[n], two[half])
         second[n].start()
-        merge_part(keep2[half])
+        merge_pair(keep2[half])
+
+    def straight_rows(start, count):
+        for r in range(count):
+            i = start + r
+            for number, target in enumerate((mean_ref, var_ref)):
+                parts = straighten([mv[number, i, t] for t in range(3)])
+                for t in range(3):
+                    target[t, pl.ds(i, 8, stride=STRIP), :] = parts[t]
 
     third = {}
-    for t, half in flows:
-        n = 2 * t + half
+    for chunk, half in flows:
+        n = 2 * chunk + half
         second[n].wait_recv()
-        kept = rows_of(half, keep1[half])
-        for index in range(6):
-            offset = index * 8
-            local = pl.multiple_of(keep2[half] * 48 + offset, 8)
-            mine = st[n, 0, pl.ds(local, 8), :]
-            other = r2[n, 0, offset : offset + 8, :]
-            gap = mine - other
-            squares = (st[n, 1, pl.ds(local, 8), :] + r2[n, 1, offset : offset + 8, :]) + gap * gap * 0.125
-            here = pl.ds(pl.multiple_of(kept + local, 8), 8)
-            mv[0, t, here, :] = (mine + other) * 0.125
-            mv[1, t, here, :] = squares * 0.125
-        block = pl.ds(pl.multiple_of(kept + keep2[half] * 48, 8), 48)
-        third[n] = remote(mv.at[:, t, block, :], mv.at[:, t, block, :], s3.at[n], q3.at[n], two[half])
+        pair = quad(chunk, half, keep1[half]) + keep2[half] * 2
+        for r in range(2):
+            local = keep2[half] * 2 + r
+            for t in range(3):
+                mine = st[n, 0, local, t]
+                other = r2[n, 0, r, t]
+                gap = mine - other
+                squares = (st[n, 1, local, t] + r2[n, 1, r, t]) + gap * gap * 0.125
+                mv[0, pair + r, t] = (mine + other) * 0.125
+                mv[1, pair + r, t] = squares * 0.125
+        block = pl.ds(pair, 2)
+        third[n] = remote(mv.at[:, block], mv.at[:, block], s3.at[n], q3.at[n], two[half])
         third[n].start()
 
     fourth = {}
-    for t, half in flows:
-        n = 2 * t + half
+    for chunk, half in flows:
+        n = 2 * chunk + half
         third[n].wait_recv()
-        kept = pl.ds(rows_of(half, keep1[half]), 96)
-        fourth[n] = remote(mv.at[:, t, kept, :], mv.at[:, t, kept, :], s4.at[n], q4.at[n], one[half])
+        kept = pl.ds(quad(chunk, half, keep1[half]), 4)
+        fourth[n] = remote(mv.at[:, kept], mv.at[:, kept], s4.at[n], q4.at[n], one[half])
         fourth[n].start()
 
-    outs = []
-    for t in range(3):
-        for half in range(2):
-            fourth[2 * t + half].wait_recv()
-        part = pl.ds(128 * t, 128)
-        for number, target in enumerate((mean_ref, var_ref)):
-            copy = pltpu.make_async_copy(mv.at[number, t], target.at[0, :, part], osem.at[number, t])
-            copy.start()
-            outs.append(copy)
-    for n in range(6):
+    for chunk, half in flows:
+        straight_rows(quad(chunk, half, keep1[half]), 4)
+    for chunk, half in flows:
+        n = 2 * chunk + half
+        fourth[n].wait_recv()
+        straight_rows(quad(chunk, half, 1 - keep1[half]), 4)
+    for copy in along_z:
+        copy.wait_send()
+    for chunk, half in flows:
+        n = 2 * chunk + half
         for m in range(2):
-            first[m, n].wait_send()
+            first(m, chunk, half).wait_send()
         second[n].wait_send()
         third[n].wait_send()
         fourth[n].wait_send()
-    for copy in outs:
-        copy.wait()
 
 
 def advance_coast(nest_host, pick, edges, source, depth):
-    shape = jax.ShapeDtypeStruct((1, 384, 384), jnp.float32)
+    shape = jax.ShapeDtypeStruct((3, 384, 128), jnp.float32)
     dma = pltpu.SemaphoreType.DMA
     return pl.pallas_call(
         coast_kernel,
         out_shape=(shape, shape),
         in_specs=[smem_spec(), smem_spec(), vmem_spec(), hbm_spec(), hbm_spec()],
-        out_specs=(hbm_spec(), hbm_spec()),
+        out_specs=(vmem_spec(), vmem_spec()),
         scratch_shapes=[
-            VMEM((X_PLANES, 2, 16, 128), jnp.float32),
-            VMEM((Z_CORES, 16, 128), jnp.float32),
-            VMEM((Z_CORES, 16, 128), jnp.float32),
-            VMEM((16, 128), jnp.float32),
+            VMEM((X_PLANES, 2, 2, 8, 128), jnp.float32),
+            VMEM((2, Z_CORES, 8, 128), jnp.float32),
+            VMEM((Z_CORES, 8, 128), jnp.float32),
+            VMEM((Z_CORES, 8, 128), jnp.float32),
+            VMEM((2, 8, 128), jnp.float32),
             VMEM((2, STRIP + 1, 3, 8, 128), jnp.float32),
             VMEM((2, STRIP, 3, 8, 128), jnp.float32),
             VMEM((2, STRIP, 3, 8, 128), jnp.float32),
@@ -714,23 +730,21 @@
             VMEM((STEPS, 2, 2, 3, 8, 128), jnp.float32),
             VMEM((2, 3, 384, 128), jnp.float32),
             VMEM((3, 384, 128), jnp.float32),
-            VMEM((2, 3, 384, 128), jnp.float32),
-            VMEM((6, 2, 96, 128), jnp.float32),
-            VMEM((6, 2, 96, 128), jnp.float32),
-            VMEM((6, 2, 48, 128), jnp.float32),
-            VMEM((2, 3, 384, 128), jnp.float32),
+            VMEM((6, 2, 4, 3, 8, 128), jnp.float32),
+            VMEM((6, 2, 4, 3, 8, 128), jnp.float32),
+            VMEM((6, 2, 2, 3, 8, 128), jnp.float32),
+            VMEM((2, STRIP, 3, 8, 128), jnp.float32),
             dma((9,)),
             dma((X_PLANES - 1,)),
             dma((X_PLANES - 1,)),
-            dma((Z_CORES - 1,)),
-            dma((Z_CORES - 1,)),
+            dma((2, Z_CORES - 1)),
+            dma((2, Z_CORES - 1)),
             dma((6, 2)),
             dma((6, 2)),
             *([dma((6,))] * 6),
-            dma((2, 3)),
         ],
         compiler_params=pltpu.CompilerParams(
-            collective_id=1, has_side_effects=True, vmem_limit_bytes=62 << 20
+            collective_id=1, has_side_effects=True, vmem_limit_bytes=40 << 20
         ),
         name="coast",
     )(nest_host, pick, edges, source, depth)
@@ -755,8 +769,9 @@
     depth = tiled(outer_depth)
     halos = exchange_halos(eta, depth)
     level, flux, edges, pick = outer_steps(wet_tiles, nest_host, nest_anchor, eta, depth, halos)
-    edges = edges.reshape(2, 16, 128)
     mean, var = advance_coast(nest_host, pick, edges, nest_source, nest_depth)
+    mean = jnp.swapaxes(mean, 0, 1).reshape(1, 384, 384)
+    var = jnp.swapaxes(var, 0, 1).reshape(1, 384, 384)
     return (untiled(level), untiled(flux), mean, var)
 
 

time: 74.7 us -> 73 us (0.977)
  Pallas kernels: 69.8 us -> 68.2 us
    pallas_call x1, Pallas kernels: 46.7 us -> 45.1 us  [advance_coast(): pl.pallas_call(coast_kernel, out_shape=(shape, shape), in_specs=[smem_spe...]
    unnamed x2 -> x12, local copies, waits for them, and re-layouts: 3.83 us -> 3.49 us
where the time goes in v5:
time: 73 us; the launch traced here: 72.9 us
  Pallas kernels  68.2 us (93%)
  local copies, waits for them, and re-layouts  3.95 us (5%)
    pallas_call x1, Pallas kernels, advance_coast(): pl.pallas_call(coast_kernel, out_shape=(shape, shape), in_specs=[smem_spe...  45.1 us
    pallas_call x1, Pallas kernels, outer_steps(): pl.pallas_call(outer_kernel, out_shape=(jax.ShapeDtypeStruct((2, 1024, 12...  12.8 us
    pallas_call x1, Pallas kernels, exchange_halos(): pl.pallas_call(halo_kernel, out_shape=(rows, rows, coef, coef), in_specs=...  10.4 us
    unnamed x12, local copies, waits for them, and re-layouts  3.49 us

profile of v5, /device:TPU:1, one launch (start us, length us, event | category | flops | bytes accessed | tf_op | source)
XLA Modules:
  0.0 72.9 jit_solution(17172028692095210707)
XLA Ops:
  0.6 0.0 copy-start.3
  0.6 0.0 copy-start.1
  0.7 0.0 copy-start
  0.7 10.4 %halo.1 = (f32[2,64,128]{2,1,0:T(8,128)}, f32[2,64,128]{2,1,0:T(8,128)}, f32[64,128]{1,0:T(8,128)}, f32[64,128]{1,0:T(8,128)}) custom-call(f32[2,1024,128]{2,1,0:T(8,128)} %bitcast.28, f32[1024,128]{1,0:T(8,128)} %bitcast.32), custom_call_target="tpu_custom_call" | custom-call | tf_op jit(solution)/shard_map/halo/pallas_call | solution.py:66
  11.0 12.8 %outer.1 = (f32[2,1024,128]{2,1,0:T(8,128)}, f32[2,2,1024,128]{3,2,1,0:T(8,128)}, f32[2,2,8,128]{3,2,1,0:T(8,128)}, s32[64]{0:T(128)}) custom-call(s32[8,64]{1,0:T(8,128)} %bitcast.34, s32[64]{0:T(128)} %host_ref.1, s32[2,64]{1,0:T(2,128)} %bitcast.35, f32[2,1024,128]{2,1,0:T(8,128)} %bitcast.29, f32[1024,128]{1,0:T(8,128)} %bitcast.33, ...), custom_call_target="tpu_custom_call" | custom-call | tf_op jit(solution)/shard_map/outer/pallas_call | solution.py:294
  23.8 0.0 copy-done.3
  23.8 0.0 copy-done.1
  23.8 0.0 copy-done
  23.8 0.0 copy-start.2
  23.8 0.7 copy-done.2
  24.5 0.0 copy-start.4
  24.5 0.7 copy-done.4
  25.2 45.1 %coast.1 = (f32[3,384,128]{2,1,0:T(8,128)S(1)}, f32[3,384,128]{2,1,0:T(8,128)S(1)}) custom-call(s32[64]{0:T(128)S(1)} %copy-done.3, s32[64]{0:T(128)S(1)} %copy-done.4, f32[2,2,8,128]{3,2,1,0:T(8,128)S(1)} %copy-done.2, f32[2,1,384,384]{3,2,1,0:T(8,128)S(1)} %copy-done, f32[1,384,384]{2,1,0:T(8,128)S(1)} %copy-done.1), custom_call_target="tpu_custom_call" | custom-call | tf_op jit(solution)/shard_map/coast/pallas_call | solution.py:713
  70.3 0.2 copy.11
  70.5 1.1 %copy.13 = f32[1,384,384]{2,1,0:T(8,128)} copy(f32[1,384,384]{1,2,0:T(8,128)S(1)} %bitcast.30) | data formatting | bytes 1179648
  71.6 0.2 copy.12
  71.8 1.1 %copy.14 = f32[1,384,384]{2,1,0:T(8,128)} copy(f32[1,384,384]{1,2,0:T(8,128)S(1)} %bitcast.31) | data formatting | bytes 1179648
Async XLA Ops:
  0.6 23.2 %copy-start.3 = (s32[64]{0:T(128)S(1)}, s32[64]{0:T(128)}, u32[]{:S(2)}) copy-start(s32[64]{0:T(128)} %host_ref.1) | copy-start | bytes 772
  0.6 23.2 %copy-start.1 = (f32[1,384,384]{2,1,0:T(8,128)S(1)}, f32[1,384,384]{2,1,0:T(8,128)}, u32[]{:S(2)}) copy-start(f32[1,384,384]{2,1,0:T(8,128)} %depth_ref.1) | copy-start | bytes 1769476
  0.7 23.2 %copy-start = (f32[2,1,384,384]{3,2,1,0:T(8,128)S(1)}, f32[2,1,384,384]{3,2,1,0:T(8,128)}, u32[]{:S(2)}) copy-start(f32[2,1,384,384]{3,2,1,0:T(8,128)} %source_ref.1) | copy-start | bytes 3538948
  23.8 0.7 copy-start.2
  24.5 0.7 copy-start.4

commit v6 on v5

--- a/solution.py
+++ b/solution.py
@@ -158,22 +158,6 @@
         for t in range(8):
             dw[i + LOW, t] = mask_of(i, t) * held(depth_in, up_depth, dn_depth, i, t)
 
-    def east_change(now):
-        rolled = [pltpu.roll(now[t], 127, 1) for t in range(8)]
-        out = []
-        for t in range(8):
-            beyond = jnp.where(lane == 127, 0.0 if t == 7 else rolled[t + 1], rolled[t])
-            out.append(beyond - now[t])
-        return out
-
-    def west_change(flow):
-        rolled = [pltpu.roll(flow[t], 1, 1) for t in range(8)]
-        out = []
-        for t in range(8):
-            behind = jnp.where(lane == 0, 0.0 if t == 0 else rolled[t - 1], rolled[t])
-            out.append(flow[t] - behind)
-        return out
-
     def place(ref, i, t, value):
         ref[pl.ds((i // 8) * 64 + t * 8 + i % 8, 8, stride=128), :] = value
 
@@ -223,61 +207,63 @@
     for copy in loads[6:]:
         copy.wait()
 
+    def level_pass(m, low, high):
+        for i in range(low, high + 1):
+            carried = 0.0
+            for t in range(8):
+                flow = fx[i + LOW, t]
+                rolled = pltpu.roll(flow, 1, 1)
+                behind = jnp.where(lane == 0, carried, rolled)
+                carried = rolled
+                down = fy[i + LOW, t] - fy[i - 1 + LOW, t]
+                now = mask_of(i, t) * (eta[i + LOW, t] - (flow - behind) - down)
+                eta[i + LOW, t] = now
+                if 0 <= i <= 15:
+                    place(levels.at[m], i, t, now)
+
+    def flux_pass(m, step, x_range, y_range):
+        for i in range(min(x_range[0], y_range[0]), max(x_range[1], y_range[1]) + 1):
+            carried = 0.0
+            for t in reversed(range(8)):
+                now = eta[i + LOW, t]
+                coef = dw[i + LOW, t]
+                if x_range[0] <= i <= x_range[1]:
+                    rolled = pltpu.roll(now, 127, 1)
+                    change = coef * (jnp.where(lane == 127, carried, rolled) - now)
+                    carried = rolled
+                    value = -change if step == 0 else fx[i + LOW, t] - change
+                    if step == 2:
+                        place(flux_out.at[0, m], i, t, value)
+                    else:
+                        fx[i + LOW, t] = value
+                if y_range[0] <= i <= y_range[1]:
+                    change = coef * (eta[i + 1 + LOW, t] - now)
+                    value = -change if step == 0 else fy[i + LOW, t] - change
+                    if step == 2:
+                        place(flux_out.at[1, m], i, t, value)
+                    else:
+                        fy[i + LOW, t] = value
+
     def member(m, _):
-        before = None
         for i in range(-2, 19):
-            now = [
-                mask_of(i, t) * held(eta_in.at[m], up_eta.at[m], dn_eta.at[m], i, t) for t in range(8)
-            ]
-            change = east_change(now) if -1 <= i <= 17 else None
             for t in range(8):
-                eta[i + LOW, t] = now[t]
+                now = mask_of(i, t) * held(eta_in.at[m], up_eta.at[m], dn_eta.at[m], i, t)
+                eta[i + LOW, t] = now
                 if 0 <= i <= 15:
-                    place(levels.at[m], i, t, now[t])
-                if change is not None:
-                    fx[i + LOW, t] = -(dw[i + LOW, t] * change[t])
-                if before is not None:
-                    fy[i - 1 + LOW, t] = -(dw[i - 1 + LOW, t] * (now[t] - before[t]))
-            before = now
+                    place(levels.at[m], i, t, now)
         edges(m, 0)
-
-        for step, low, high in ((1, -1, 17), (2, 0, 16)):
-            before = None
-            flow_before = [fy[low - 1 + LOW, t] for t in range(8)]
-            for i in range(low, high + 1):
-                px = [fx[i + LOW, t] for t in range(8)]
-                py = [fy[i + LOW, t] for t in range(8)]
-                leave = west_change(px)
-                now = [
-                    mask_of(i, t) * (eta[i + LOW, t] - leave[t] - (py[t] - flow_before[t])) for t in range(8)
-                ]
-                change = east_change(now) if (0 if step == 1 else low) <= i < high or step == 1 else None
-                for t in range(8):
-                    if step == 1:
-                        eta[i + LOW, t] = now[t]
-                    if 0 <= i <= 15:
-                        place(levels.at[m], i, t, now[t])
-                    if change is not None:
-                        value = px[t] - dw[i + LOW, t] * change[t]
-                        if step == 1:
-                            fx[i + LOW, t] = value
-                        else:
-                            place(flux_out.at[0, m], i, t, value)
-                    if before is not None:
-                        value = flow_before[t] - dw[i - 1 + LOW, t] * (now[t] - before[t])
-                        if step == 1:
-                            fy[i - 1 + LOW, t] = value
-                        else:
-                            place(flux_out.at[1, m], i - 1, t, value)
-                before = now
-                flow_before = py
-            if step == 2:
-                pltpu.make_async_copy(levels.at[m], level_hbm.at[m], out_sem.at[0, m]).start()
-                for side in range(2):
-                    pltpu.make_async_copy(
-                        flux_out.at[side, m], flux_hbm.at[side, m], out_sem.at[1 + side, m]
-                    ).start()
-            edges(m, step)
+        flux_pass(m, 0, (-1, 17), (-2, 17))
+        level_pass(m, -1, 17)
+        edges(m, 1)
+        flux_pass(m, 1, (0, 16), (-1, 16))
+        level_pass(m, 0, 16)
+        pltpu.make_async_copy(levels.at[m], level_hbm.at[m], out_sem.at[0, m]).start()
+        flux_pass(m, 2, (0, 15), (0, 15))
+        for side in range(2):
+            pltpu.make_async_copy(
+                flux_out.at[side, m], flux_hbm.at[side, m], out_sem.at[1 + side, m]
+            ).start()
+        edges(m, 2)
         return 0
 
     lax.fori_loop(0, 2, member, 0)
@@ -744,10 +730,35 @@
             *([dma((6,))] * 6),
         ],
         compiler_params=pltpu.CompilerParams(
-            collective_id=1, has_side_effects=True, vmem_limit_bytes=40 << 20
+            collective_id=1, has_side_effects=True, vmem_limit_bytes=62 << 20
         ),
         name="coast",
     )(nest_host, pick, edges, source, depth)
+
+
+def emit_kernel(mean_ref, var_ref, mean_hbm, var_hbm, sem):
+    copies = []
+    for number, (source, target) in enumerate(((mean_ref, mean_hbm), (var_ref, var_hbm))):
+        for t in range(3):
+            copy = pltpu.make_async_copy(
+                source.at[t], target.at[0, :, pl.ds(128 * t, 128)], sem.at[number, t]
+            )
+            copy.start()
+            copies.append(copy)
+    for copy in copies:
+        copy.wait()
+
+
+def emit(mean, var):
+    shape = jax.ShapeDtypeStruct((1, 384, 384), jnp.float32)
+    return pl.pallas_call(
+        emit_kernel,
+        out_shape=(shape, shape),
+        in_specs=[vmem_spec()] * 2,
+        out_specs=(hbm_spec(), hbm_spec()),
+        scratch_shapes=[pltpu.SemaphoreType.DMA((2, 3))],
+        name="emit",
+    )(mean, var)
 
 
 def tiled(field):
@@ -770,8 +781,7 @@
     halos = exchange_halos(eta, depth)
     level, flux, edges, pick = outer_steps(wet_tiles, nest_host, nest_anchor, eta, depth, halos)
     mean, var = advance_coast(nest_host, pick, edges, nest_source, nest_depth)
-    mean = jnp.swapaxes(mean, 0, 1).reshape(1, 384, 384)
-    var = jnp.swapaxes(var, 0, 1).reshape(1, 384, 384)
+    mean, var = emit(mean, var)
     return (untiled(level), untiled(flux), mean, var)
 
 

time: 73 us -> 70.1 us (0.960)
  local copies, waits for them, and re-layouts: 3.95 us -> 0 us
  Pallas kernels: 68.2 us -> 69.2 us
    unnamed x12 -> x0, local copies, waits for them, and re-layouts: 3.49 us -> none
    pallas_call x1, Pallas kernels: 12.8 us -> 10 us  [outer_steps(): pl.pallas_call(outer_kernel, out_shape=(jax.ShapeDtypeStruct((2, 1024, 12...]
    pallas_call x0 -> x1, Pallas kernels: none -> 2.29 us  [emit(): pl.pallas_call(emit_kernel, out_shape=(shape, shape), in_specs=[vmem_spec...]
    pallas_call x1, Pallas kernels: 45.1 us -> 46.5 us  [advance_coast(): pl.pallas_call(coast_kernel, out_shape=(shape, shape), in_specs=[smem_spe...]
where the time goes in v6:
time: 70.1 us; the launch traced here: 69.9 us
  Pallas kernels  69.2 us (99%)
    pallas_call x1, Pallas kernels, advance_coast(): pl.pallas_call(coast_kernel, out_shape=(shape, shape), in_specs=[smem_spe...  46.5 us
    pallas_call x1, Pallas kernels, exchange_halos(): pl.pallas_call(halo_kernel, out_shape=(rows, rows, coef, coef), in_specs=...  10.4 us
    pallas_call x1, Pallas kernels, outer_steps(): pl.pallas_call(outer_kernel, out_shape=(jax.ShapeDtypeStruct((2, 1024, 12...  10 us
    pallas_call x1, Pallas kernels, emit(): pl.pallas_call(emit_kernel, out_shape=(shape, shape), in_specs=[vmem_spec...  2.29 us

profile of v6, /device:TPU:1, one launch (start us, length us, event | category | flops | bytes accessed | tf_op | source)
XLA Modules:
  0.0 69.9 jit_solution(6983132982826843650)
XLA Ops:
  0.6 10.4 %halo.1 = (f32[2,64,128]{2,1,0:T(8,128)}, f32[2,64,128]{2,1,0:T(8,128)}, f32[64,128]{1,0:T(8,128)}, f32[64,128]{1,0:T(8,128)}) custom-call(f32[2,1024,128]{2,1,0:T(8,128)} %bitcast.22, f32[1024,128]{1,0:T(8,128)} %bitcast.24), custom_call_target="tpu_custom_call" | custom-call | tf_op jit(solution)/shard_map/halo/pallas_call | solution.py:66
  11.0 10.0 %outer.1 = (f32[2,1024,128]{2,1,0:T(8,128)}, f32[2,2,1024,128]{3,2,1,0:T(8,128)}, f32[2,2,8,128]{3,2,1,0:T(8,128)}, s32[64]{0:T(128)}) custom-call(s32[8,64]{1,0:T(8,128)} %bitcast.26, s32[64]{0:T(128)} %host_ref.1, s32[2,64]{1,0:T(2,128)} %bitcast.27, f32[2,1024,128]{2,1,0:T(8,128)} %bitcast.23, f32[1024,128]{1,0:T(8,128)} %bitcast.25, ...), custom_call_target="tpu_custom_call" | custom-call | tf_op jit(solution)/shard_map/outer/pallas_call | solution.py:280
  21.0 46.5 %coast.1 = (f32[3,384,128]{2,1,0:T(8,128)}, f32[3,384,128]{2,1,0:T(8,128)}) custom-call(s32[64]{0:T(128)} %host_ref.1, s32[64]{0:T(128)} %get-tuple-element.22.pick_ref, f32[2,2,8,128]{3,2,1,0:T(8,128)} %get-tuple-element.23.edges_ref, f32[2,1,384,384]{3,2,1,0:T(8,128)} %source_ref.1, f32[1,384,384]{2,1,0:T(8,128)} %depth_ref.1), custom_call_target="tpu_custom_call" | custom-call | tf_op jit(solution)/shard_map/coast/pallas_call | solution.py:699
  67.6 2.3 %emit.1 = (f32[1,384,384]{2,1,0:T(8,128)}, f32[1,384,384]{2,1,0:T(8,128)}) custom-call(f32[3,384,128]{2,1,0:T(8,128)} %get-tuple-element.24.mean_ref, f32[3,384,128]{2,1,0:T(8,128)} %get-tuple-element.25.var_ref), custom_call_target="tpu_custom_call" | custom-call | tf_op jit(solution)/shard_map/emit/pallas_call | solution.py:754

commit v7 on v6

--- a/solution.py
+++ b/solution.py
@@ -9,8 +9,9 @@
 STEPS = 3
 REFINE = 6
 SECTIONS = 64
-X_PLANES = 4
 Z_CORES = 16
+Z_LINE = 8
+GROUP = 8
 STRIP = 48
 BATCH = 48
 VMEM = pltpu.VMEM
@@ -121,7 +122,8 @@
 
     def choose(n, _):
         section_of = host[n]
-        pick_ref[n] = (section_of // Z_CORES) * 2 + jnp.where(first[section_of] == n, 0, 1)
+        group = (section_of // Z_CORES) * 2 + lax.rem(section_of, 2)
+        pick_ref[n] = group * 2 + jnp.where(first[section_of] == n, 0, 1)
         return 0
 
     lax.fori_loop(0, SECTIONS, choose, 0, unroll=8)
@@ -489,7 +491,9 @@
 ):
     sec = lax.axis_index("sec")
     plane = sec // Z_CORES
-    spot = lax.rem(sec, Z_CORES)
+    core = lax.rem(sec, 2)
+    spot = lax.rem(sec, Z_CORES) // 2
+    group = plane * 2 + core
     mem = lax.axis_index("mem")
     near = mem + 1 - 2 * lax.rem(mem, 2)
     far = 3 - mem
@@ -511,42 +515,48 @@
     for copy in loads:
         copy.start()
 
+    def in_group(step):
+        other = lax.rem(group + step, GROUP)
+        return (other // 2) * Z_CORES + spot * 2 + lax.rem(other, 2)
+
+    def in_line(step):
+        return plane * Z_CORES + lax.rem(spot + step, Z_LINE) * 2 + core
+
     barrier = pltpu.get_barrier_semaphore()
-    for step in range(1, X_PLANES):
-        peer = lax.rem(plane + step, X_PLANES) * Z_CORES + spot
-        pl.semaphore_signal(barrier, inc=1, device_id={"sec": peer}, device_id_type=MESH)
-    for step in range(1, Z_CORES):
-        peer = plane * Z_CORES + lax.rem(spot + step, Z_CORES)
-        pl.semaphore_signal(barrier, inc=1, device_id={"sec": peer}, device_id_type=MESH)
+    for step in range(1, GROUP):
+        pl.semaphore_signal(barrier, inc=1, device_id={"sec": in_group(step)}, device_id_type=MESH)
+    for step in range(1, Z_LINE):
+        pl.semaphore_signal(barrier, inc=1, device_id={"sec": in_line(step)}, device_id_type=MESH)
     for peer in (near, far):
         pl.semaphore_signal(barrier, inc=1, device_id={"mem": peer}, device_id_type=MESH)
-    gathered[plane] = edges_ref[...]
-    pl.semaphore_wait(barrier, X_PLANES + Z_CORES)
+    for copy in loads[:3]:
+        copy.wait()
+    load_depth(dsrc, coef, d2)
+    gathered[group] = edges_ref[...]
+    pl.semaphore_wait(barrier, GROUP + Z_LINE)
 
     along_x = []
-    for step in range(1, X_PLANES):
-        peer = lax.rem(plane + step, X_PLANES) * Z_CORES + spot
+    for step in range(1, GROUP):
         copy = pltpu.make_async_remote_copy(
             src_ref=edges_ref,
-            dst_ref=gathered.at[plane],
+            dst_ref=gathered.at[group],
             send_sem=send_x.at[step - 1],
             recv_sem=recv_x.at[step - 1],
-            device_id={"sec": peer},
+            device_id={"sec": in_group(step)},
             device_id_type=MESH,
         )
         copy.start()
         along_x.append(copy)
-    for copy in loads[:3]:
+    for copy in loads[3:]:
         copy.wait()
-    load_depth(dsrc, coef, d2)
+    load_source(src, h, div, 0)
     for copy in along_x:
         copy.wait()
     along_z = []
     incoming = (incoming_first, incoming_later)
     for part in range(2):
-        for step in range(Z_CORES):
-            target = lax.rem(spot + step, Z_CORES)
-            choice = pick_ref[plane * Z_CORES + target]
+        for step in range(Z_LINE):
+            choice = pick_ref[in_line(step)]
             message = gathered[choice // 2, lax.rem(choice, 2), part]
             if step == 0:
                 incoming[part][spot] = message
@@ -557,17 +567,14 @@
                 dst_ref=incoming[part].at[spot],
                 send_sem=send_z.at[part, step - 1],
                 recv_sem=recv_z.at[part, step - 1],
-                device_id={"sec": plane * Z_CORES + target},
+                device_id={"sec": in_line(step)},
                 device_id_type=MESH,
             )
             copy.start()
             along_z.append(copy)
-    for copy in loads[3:]:
-        copy.wait()
-    for m in range(2):
-        load_source(src, h, div, m)
-    host_spot = lax.rem(host_ref[sec], Z_CORES)
-    for copy in along_z[: Z_CORES - 1]:
+    load_source(src, h, div, 1)
+    host_spot = lax.rem(host_ref[sec], Z_CORES) // 2
+    for copy in along_z[: Z_LINE - 1]:
         copy.wait_recv()
     own_edge[0] = incoming_first[host_spot]
     spread_edges(own_edge.at[0], cols, rows, (0,))
@@ -578,7 +585,7 @@
         return 0
 
     lax.fori_loop(0, 2, early, 0)
-    for copy in along_z[Z_CORES - 1 :]:
+    for copy in along_z[Z_LINE - 1 :]:
         copy.wait_recv()
     own_edge[1] = incoming_later[host_spot]
     spread_edges(own_edge.at[1], cols, rows, (1, 2))
@@ -702,10 +709,10 @@
         in_specs=[smem_spec(), smem_spec(), vmem_spec(), hbm_spec(), hbm_spec()],
         out_specs=(vmem_spec(), vmem_spec()),
         scratch_shapes=[
-            VMEM((X_PLANES, 2, 2, 8, 128), jnp.float32),
-            VMEM((2, Z_CORES, 8, 128), jnp.float32),
-            VMEM((Z_CORES, 8, 128), jnp.float32),
-            VMEM((Z_CORES, 8, 128), jnp.float32),
+            VMEM((GROUP, 2, 2, 8, 128), jnp.float32),
+            VMEM((2, Z_LINE, 8, 128), jnp.float32),
+            VMEM((Z_LINE, 8, 128), jnp.float32),
+            VMEM((Z_LINE, 8, 128), jnp.float32),
             VMEM((2, 8, 128), jnp.float32),
             VMEM((2, STRIP + 1, 3, 8, 128), jnp.float32),
             VMEM((2, STRIP, 3, 8, 128), jnp.float32),
@@ -721,10 +728,10 @@
             VMEM((6, 2, 2, 3, 8, 128), jnp.float32),
             VMEM((2, STRIP, 3, 8, 128), jnp.float32),
             dma((9,)),
-            dma((X_PLANES - 1,)),
-            dma((X_PLANES - 1,)),
-            dma((2, Z_CORES - 1)),
-            dma((2, Z_CORES - 1)),
+            dma((GROUP - 1,)),
+            dma((GROUP - 1,)),
+            dma((2, Z_LINE - 1)),
+            dma((2, Z_LINE - 1)),
             dma((6, 2)),
             dma((6, 2)),
             *([dma((6,))] * 6),

time: 70.1 us -> 68.8 us (0.981); the launches traced: 69.9 us -> 67.7 us
  Pallas kernels: 69.2 us -> 67.1 us
    pallas_call x1, Pallas kernels: 46.5 us -> 44.2 us  [advance_coast(): pl.pallas_call(coast_kernel, out_shape=(shape, shape), in_specs=[smem_spe...]
where the time goes in v7:
time: 68.8 us; the launch traced here: 67.7 us
  Pallas kernels  67.1 us (98%)
    pallas_call x1, Pallas kernels, advance_coast(): pl.pallas_call(coast_kernel, out_shape=(shape, shape), in_specs=[smem_spe...  44.2 us
    pallas_call x1, Pallas kernels, exchange_halos(): pl.pallas_call(halo_kernel, out_shape=(rows, rows, coef, coef), in_specs=...  10.4 us
    pallas_call x1, Pallas kernels, outer_steps(): pl.pallas_call(outer_kernel, out_shape=(jax.ShapeDtypeStruct((2, 1024, 12...  10.2 us
    pallas_call x1, Pallas kernels, emit(): pl.pallas_call(emit_kernel, out_shape=(shape, shape), in_specs=[vmem_spec...  2.29 us

profile of v7, /device:TPU:1, one launch (start us, length us, event | category | flops | bytes accessed | tf_op | source)
XLA Modules:
  0.0 67.7 jit_solution(9330380421110088205)
XLA Ops:
  0.6 10.4 %halo.1 = (f32[2,64,128]{2,1,0:T(8,128)}, f32[2,64,128]{2,1,0:T(8,128)}, f32[64,128]{1,0:T(8,128)}, f32[64,128]{1,0:T(8,128)}) custom-call(f32[2,1024,128]{2,1,0:T(8,128)} %bitcast.22, f32[1024,128]{1,0:T(8,128)} %bitcast.24), custom_call_target="tpu_custom_call" | custom-call | tf_op jit(solution)/shard_map/halo/pallas_call | solution.py:67
  11.0 10.2 %outer.1 = (f32[2,1024,128]{2,1,0:T(8,128)}, f32[2,2,1024,128]{3,2,1,0:T(8,128)}, f32[2,2,8,128]{3,2,1,0:T(8,128)}, s32[64]{0:T(128)}) custom-call(s32[8,64]{1,0:T(8,128)} %bitcast.26, s32[64]{0:T(128)} %host_ref.1, s32[2,64]{1,0:T(2,128)} %bitcast.27, f32[2,1024,128]{2,1,0:T(8,128)} %bitcast.23, f32[1024,128]{1,0:T(8,128)} %bitcast.25, ...), custom_call_target="tpu_custom_call" | custom-call | tf_op jit(solution)/shard_map/outer/pallas_call | solution.py:282
  21.2 44.2 %coast.1 = (f32[3,384,128]{2,1,0:T(8,128)}, f32[3,384,128]{2,1,0:T(8,128)}) custom-call(s32[64]{0:T(128)} %host_ref.1, s32[64]{0:T(128)} %get-tuple-element.22.pick_ref, f32[2,2,8,128]{3,2,1,0:T(8,128)} %get-tuple-element.23.edges_ref, f32[2,1,384,384]{3,2,1,0:T(8,128)} %source_ref.1, f32[1,384,384]{2,1,0:T(8,128)} %depth_ref.1), custom_call_target="tpu_custom_call" | custom-call | tf_op jit(solution)/shard_map/coast/pallas_call | solution.py:706
  65.4 2.3 %emit.1 = (f32[1,384,384]{2,1,0:T(8,128)}, f32[1,384,384]{2,1,0:T(8,128)}) custom-call(f32[3,384,128]{2,1,0:T(8,128)} %get-tuple-element.24.mean_ref, f32[3,384,128]{2,1,0:T(8,128)} %get-tuple-element.25.var_ref), custom_call_target="tpu_custom_call" | custom-call | tf_op jit(solution)/shard_map/emit/pallas_call | solution.py:761

commit v8 on v7

--- a/solution.py
+++ b/solution.py
@@ -743,16 +743,28 @@
     )(nest_host, pick, edges, source, depth)
 
 
-def emit_kernel(mean_ref, var_ref, mean_hbm, var_hbm, sem):
-    copies = []
-    for number, (source, target) in enumerate(((mean_ref, mean_hbm), (var_ref, var_hbm))):
-        for t in range(3):
-            copy = pltpu.make_async_copy(
-                source.at[t], target.at[0, :, pl.ds(128 * t, 128)], sem.at[number, t]
-            )
-            copy.start()
-            copies.append(copy)
-    for copy in copies:
+def emit_kernel(mean_ref, var_ref, mean_hbm, var_hbm, held, in_sem, out_sem):
+    parts = [
+        (number, t, source, target)
+        for number, (source, target) in enumerate(((mean_ref, mean_hbm), (var_ref, var_hbm)))
+        for t in range(3)
+    ]
+    loads = [
+        pltpu.make_async_copy(source.at[t], held.at[number, t], in_sem.at[number, t])
+        for number, t, source, _ in parts
+    ]
+    stores = [
+        pltpu.make_async_copy(
+            held.at[number, t], target.at[0, :, pl.ds(128 * t, 128)], out_sem.at[number, t]
+        )
+        for number, t, _, target in parts
+    ]
+    for copy in loads:
+        copy.start()
+    for load, store in zip(loads, stores):
+        load.wait()
+        store.start()
+    for copy in stores:
         copy.wait()
 
 
@@ -761,9 +773,14 @@
     return pl.pallas_call(
         emit_kernel,
         out_shape=(shape, shape),
-        in_specs=[vmem_spec()] * 2,
+        in_specs=[hbm_spec()] * 2,
         out_specs=(hbm_spec(), hbm_spec()),
-        scratch_shapes=[pltpu.SemaphoreType.DMA((2, 3))],
+        scratch_shapes=[
+            VMEM((2, 3, 384, 128), jnp.float32),
+            pltpu.SemaphoreType.DMA((2, 3)),
+            pltpu.SemaphoreType.DMA((2, 3)),
+        ],
+        compiler_params=pltpu.CompilerParams(vmem_limit_bytes=62 << 20),
         name="emit",
     )(mean, var)
 

time: 68.8 us -> 68.7 us (level)
  no operation moved by 1% of the time
where the time goes in v8:
time: 68.7 us; the launch traced here: 67.5 us
  Pallas kernels  66.9 us (97%)
    pallas_call x1, Pallas kernels, advance_coast(): pl.pallas_call(coast_kernel, out_shape=(shape, shape), in_specs=[smem_spe...  44.3 us
    pallas_call x1, Pallas kernels, exchange_halos(): pl.pallas_call(halo_kernel, out_shape=(rows, rows, coef, coef), in_specs=...  10.4 us
    pallas_call x1, Pallas kernels, outer_steps(): pl.pallas_call(outer_kernel, out_shape=(jax.ShapeDtypeStruct((2, 1024, 12...  10.1 us
    pallas_call x1, Pallas kernels, emit(): pl.pallas_call(emit_kernel, out_shape=(shape, shape), in_specs=[hbm_spec(...  2.13 us

profile of v8, /device:TPU:1, one launch (start us, length us, event | category | flops | bytes accessed | tf_op | source)
XLA Modules:
  0.0 67.5 jit_solution(8309219487753507317)
XLA Ops:
  0.6 10.4 %halo.1 = (f32[2,64,128]{2,1,0:T(8,128)}, f32[2,64,128]{2,1,0:T(8,128)}, f32[64,128]{1,0:T(8,128)}, f32[64,128]{1,0:T(8,128)}) custom-call(f32[2,1024,128]{2,1,0:T(8,128)} %bitcast.22, f32[1024,128]{1,0:T(8,128)} %bitcast.24), custom_call_target="tpu_custom_call" | custom-call | tf_op jit(solution)/shard_map/halo/pallas_call | solution.py:67
  11.0 10.1 %outer.1 = (f32[2,1024,128]{2,1,0:T(8,128)}, f32[2,2,1024,128]{3,2,1,0:T(8,128)}, f32[2,2,8,128]{3,2,1,0:T(8,128)}, s32[64]{0:T(128)}) custom-call(s32[8,64]{1,0:T(8,128)} %bitcast.26, s32[64]{0:T(128)} %host_ref.1, s32[2,64]{1,0:T(2,128)} %bitcast.27, f32[2,1024,128]{2,1,0:T(8,128)} %bitcast.23, f32[1024,128]{1,0:T(8,128)} %bitcast.25, ...), custom_call_target="tpu_custom_call" | custom-call | tf_op jit(solution)/shard_map/outer/pallas_call | solution.py:282
  21.1 44.3 %coast.1 = (f32[3,384,128]{2,1,0:T(8,128)}, f32[3,384,128]{2,1,0:T(8,128)}) custom-call(s32[64]{0:T(128)} %host_ref.1, s32[64]{0:T(128)} %get-tuple-element.22.pick_ref, f32[2,2,8,128]{3,2,1,0:T(8,128)} %get-tuple-element.23.edges_ref, f32[2,1,384,384]{3,2,1,0:T(8,128)} %source_ref.1, f32[1,384,384]{2,1,0:T(8,128)} %depth_ref.1), custom_call_target="tpu_custom_call" | custom-call | tf_op jit(solution)/shard_map/coast/pallas_call | solution.py:706
  65.4 2.1 %emit.1 = (f32[1,384,384]{2,1,0:T(8,128)}, f32[1,384,384]{2,1,0:T(8,128)}) custom-call(f32[3,384,128]{2,1,0:T(8,128)} %get-tuple-element.24.mean_ref, f32[3,384,128]{2,1,0:T(8,128)} %get-tuple-element.25.var_ref), custom_call_target="tpu_custom_call" | custom-call | tf_op jit(solution)/shard_map/emit/pallas_call | solution.py:773
